TPU v7x, 1024 devices: a whole 4x4x32 slice. The times are simulated.
1024 devices in a mesh: row: 16 (over x, y), col: 64 (over z, core).
Axes of the slice: x: 4, y: 4, z: 32, core: 2. Of those that a mesh axis runs over, the one named last changes fastest.
Arguments:
- omega_sq: float32 [8192, 8192], P('row', 'col'), may hold values from -6 to 6
- pole_freq: float32 [8192, 8192], P('row', 'col'), may hold values from 0.5 to 4
- mtx_left: float32 [1, 8192, 128], P(None, ('row', 'col')), may hold values from -0.0625 to 0.0625
- mtx_right: float32 [1, 8192, 128], P(None, ('col', 'row')), may hold values from -0.0625 to 0.0625
- band_ids: int32 [1], replicated, may hold values from 0 to 63
- band_energy: float32 [64], replicated, may hold values from -3 to 1
- eval_energy: float32 [3], replicated, may hold values from -1 to 1
Outputs:
- sigma: float32 [128, 384], replicated
All inputs are finite; a program needn't handle non-finite values.
Results may differ from a plain program's by a relative error of at most 0.0001.
Values sent between devices are 32-bit elements; how exact they have to be, the bound alone decides.
No kernel may reach another device: no remote copies, remote signals or barrier semaphores. Data moves between devices by JAX's collectives and lax.ppermute only.
A program may use at most 32 MiB of HBM per device.

v0:
```python
import jax
import jax.numpy as jnp
from jax import lax
from jax.sharding import PartitionSpec as P


def contract_rows(left, right):
    return lax.dot_general(
        left,
        right,
        (((0,), (0,)), ((), ())),
        precision=lax.Precision.HIGHEST,
        preferred_element_type=jnp.float32,
    )


def kernel_rows(ratio, freq, shift_row, right_cols, energies):
    parts = []
    for energy in range(energies):
        gap = shift_row[energy] - freq
        kern = ratio * gap / (gap * gap + 0.09)
        parts.append(
            jnp.dot(
                kern,
                right_cols,
                preferred_element_type=jnp.float32,
                precision=lax.Precision.HIGHEST,
            )
        )
    return jnp.concatenate(parts, axis=1)


def shards(omega_sq, pole_freq, mtx_left, mtx_right, band_ids, band_energy, eval_energy):
    table = band_energy.shape[0]
    energies = eval_energy.shape[0]
    hits = (band_ids[:, None] == jnp.arange(table, dtype=jnp.int32)[None, :]).astype(jnp.float32)
    levels = jnp.sum(hits * band_energy[None, :], axis=1)
    shifts = eval_energy[None, :] - levels[:, None]
    ratio = omega_sq / pole_freq
    shift_row = shifts[0]
    right_cols = lax.all_gather(mtx_right[0], "row", axis=0, tiled=True)
    product = kernel_rows(ratio, pole_freq, shift_row, right_cols, energies)
    total = contract_rows(lax.all_gather(mtx_left[0], "col", axis=0, tiled=True), product)
    return lax.psum(total, ("row", "col"))


def solution(mesh):
    return jax.shard_map(
        shards,
        mesh=mesh,
        in_specs=(
            P("row", "col"),
            P("row", "col"),
            P(None, ("row", "col"), None),
            P(None, ("col", "row"), None),
            P(),
            P(),
            P(),
        ),
        out_specs=P(),
        check_vma=False,
    )
```

profile of v0, /device:TPU:1, one launch (start us, length us, event | category | flops | bytes accessed | tf_op | source)
XLA Modules:
  0.0 985.6 jit_solution(12755472601016205351)
XLA Ops:
  6.5 0.0 all-reduce.2.cloned.1.call-start
  6.5 0.0 copy-start.4
  6.5 0.0 copy-start.5
  7.2 0.0 copy-start.1
  7.2 0.0 copy-done.4
  7.2 0.6 fusion.33
  7.8 0.0 copy-done.5
  7.9 0.6 subtract_bitcast_fusion
  8.5 0.6 fusion.41
  9.1 0.0 copy-done.1
  9.1 19.3 %all-gather = f32[1,128,128]{2,1,0:T(8,128)S(1)} all-gather(f32[1,8,128]{2,1,0:T(8,128)S(1)} %copy-done.1), channel_id=2, replica_groups=mesh['row'=16,'col'=64] {'row'}, dimensions={1}, use_global_device_ids=true | all-gather | bytes 69632 | tf_op jit(solution)/shard_map/all_gather | solution.py:41
  28.4 0.0 copy-start.2
  28.4 0.0 copy-start.3
  28.4 2.0 fusion.12
  30.5 0.0 copy-done.2
  30.5 0.0 copy-done.3
  30.5 1.0 fusion.6
  31.5 0.0 copy-start
  31.5 1.0 fusion.18
  32.6 0.0 copy-done
  32.6 75.5 %all-gather.1 = f32[1,512,128]{2,1,0:T(8,128)S(1)} all-gather(f32[1,8,128]{2,1,0:T(8,128)S(1)} %copy-done), channel_id=3, replica_groups=mesh['row'=16,'col'=64] {'col'}, dimensions={1}, use_global_device_ids=true | all-gather | bytes 266240 | tf_op jit(solution)/shard_map/all_gather | solution.py:43
  108.1 2.1 convolution_bitcast_fusion
  110.2 0.0 all-reduce.2.cloned.1.call-update
  110.2 866.8 %all-reduce.2.cloned.1.call-done = f32[128,384]{0,1:T(8,128)} async-done(((f32[128,384]{0,1:T(8,128)}), f32[128,384]{0,1:T(8,128)}) %all-reduce.2.cloned.1.call-update) | async-done | bytes 196624 | tf_op jit(solution)/shard_map/psum | solution.py:44
  977.0 1.7 copy.8
Async XLA Ops:
  6.5 970.5 %all-reduce.2.cloned.1.call-start = ((), (), s32[]{:S(2)}) async-start(), calls=%async_computation | async-start | bytes 393216 | tf_op jit(solution)/shard_map/psum | solution.py:44
  6.5 0.7 copy-start.4
  6.5 1.3 copy-start.5
  7.2 1.9 copy-start.1
  28.4 2.1 copy-start.2
  28.4 2.1 copy-start.3
  31.5 1.1 copy-start
Sparse Core Ops, SparseCore 0:
  110.3 866.6 all-reduce.1
where the time goes:
time: 986 us
  waiting for transfers between devices  867 us (88%)
  blocking collectives  94.9 us (10%)
  between operations  14.2 us (1%)
    psum x1, waiting for transfers between devices, shards(): return lax.psum(total, ('row', 'col'))  867 us
    all_gather x1, blocking collectives, shards(): lax.all_gather(mtx_left[0], 'col', axis=0, tiled=True)  75.5 us
  transfers between devices with their start and end apart: 1, of which 1 were waited for; matrix products, arithmetic and copies ran while one was open for 0% of the time, Pallas kernels for 0%

commit v1 on v0

--- a/solution.py
+++ b/solution.py
@@ -1,7 +1,10 @@
 import jax
 import jax.numpy as jnp
 from jax import lax
-from jax.sharding import PartitionSpec as P
+from jax.sharding import Mesh, PartitionSpec as P
+
+ROW = ("x", "y")
+COL = ("z_hi", "z_mid", "z_lo", "core")
 
 
 def contract_rows(left, right):
@@ -30,29 +33,47 @@
     return jnp.concatenate(parts, axis=1)
 
 
+def gather(block, axes):
+    size = lax.axis_size(axes)
+    return lax.all_to_all(jnp.broadcast_to(block, (size, *block.shape)), axes, 0, 0)
+
+
+def sum_everywhere(total, near, far):
+    rows, columns = total.shape
+    size = lax.axis_size(near)
+    pieces = lax.all_to_all(total.reshape(size, rows // size, columns), near, 0, 0)
+    piece = jnp.sum(gather(jnp.sum(pieces, axis=0), far), axis=0)
+    return gather(piece, near).reshape(rows, columns)
+
+
 def shards(omega_sq, pole_freq, mtx_left, mtx_right, band_ids, band_energy, eval_energy):
     table = band_energy.shape[0]
     energies = eval_energy.shape[0]
+    states = mtx_left.shape[2]
     hits = (band_ids[:, None] == jnp.arange(table, dtype=jnp.int32)[None, :]).astype(jnp.float32)
     levels = jnp.sum(hits * band_energy[None, :], axis=1)
     shifts = eval_energy[None, :] - levels[:, None]
+    left_far = gather(mtx_left[0], ("z_hi", "z_mid"))
+    left_near = gather(left_far, ("z_lo", "core"))
+    left_rows = jnp.transpose(left_near, (1, 0, 2, 3)).reshape(-1, states)
     ratio = omega_sq / pole_freq
     shift_row = shifts[0]
-    right_cols = lax.all_gather(mtx_right[0], "row", axis=0, tiled=True)
+    right_cols = gather(mtx_right[0], ROW).reshape(-1, states)
     product = kernel_rows(ratio, pole_freq, shift_row, right_cols, energies)
-    total = contract_rows(lax.all_gather(mtx_left[0], "col", axis=0, tiled=True), product)
-    return lax.psum(total, ("row", "col"))
+    total = contract_rows(left_rows, product)
+    return sum_everywhere(total, (*ROW, "z_lo", "core"), ("z_hi", "z_mid"))
 
 
 def solution(mesh):
+    split = Mesh(mesh.devices.reshape(4, 4, 8, 2, 2, 2), (*ROW, *COL))
     return jax.shard_map(
         shards,
-        mesh=mesh,
+        mesh=split,
         in_specs=(
-            P("row", "col"),
-            P("row", "col"),
-            P(None, ("row", "col"), None),
-            P(None, ("col", "row"), None),
+            P(ROW, COL),
+            P(ROW, COL),
+            P(None, (*ROW, *COL), None),
+            P(None, (*COL, *ROW), None),
             P(),
             P(),
             P(),

time: 986 us -> 136 us (0.14)
  waiting for transfers between devices: 867 us -> 0.01 us
  blocking collectives: 94.9 us -> 118 us
  between operations: 14.2 us -> 0.74 us
    psum x1 -> x0, waiting for transfers between devices: 867 us -> none  [shards(): return lax.psum(total, ('row', 'col'))]
    all_to_all x0 -> x5, blocking collectives: none -> 118 us  [the longest x4 103 us: gather(): lax.all_to_all(jnp.broadcast_to(block, (size, *block.shape)), axes, 0, 0)]
    all_gather x2 -> x0, blocking collectives: 94.9 us -> none  [the longest x1 75.5 us: shards(): lax.all_gather(mtx_left[0], 'col', axis=0, tiled=True)]
  transfers between devices with their start and end apart: 1 -> 1, of which waited for: 1 -> 0; matrix products, arithmetic and copies ran while one was open for 0% -> 4% of each run, Pallas kernels for 0% -> 0%
where the time goes in v1:
time: 136 us; the launch traced here: 135 us
  blocking collectives  118 us (87%)
  starting transfers between devices  7.13 us (5%)
  matrix products  4.18 us (3%)
  local copies, waits for them, and re-layouts  3.73 us (3%)
  other arithmetic  1.41 us (1%)
    all_to_all x4, blocking collectives, gather(): lax.all_to_all(jnp.broadcast_to(block, (size, *block.shape)), axes, 0, 0)  103 us
    all_to_all x1, blocking collectives, sum_everywhere(): lax.all_to_all(total.reshape(size, rows // size, columns), near, 0, 0)  14.6 us
    all_to_all x1, starting transfers between devices, gather(): lax.all_to_all(jnp.broadcast_to(block, (size, *block.shape)), axes, 0, 0)  7.13 us
    dot_general x3, matrix products, kernel_rows(): jnp.dot(kern, right_cols, preferred_element_type=jnp.float32, precision=l...  3.29 us
  transfers between devices with their start and end apart: 1, of which 0 were waited for; matrix products, arithmetic and copies ran while one was open for 4% of the time, Pallas kernels for 0%

profile of v1, /device:TPU:1, one launch (start us, length us, event | category | flops | bytes accessed | tf_op | source)
XLA Modules:
  0.0 135.1 jit_solution(7683074031721078856)
XLA Ops:
  0.0 0.7 broadcast_in_dim.20
  0.7 0.0 copy-start
  0.7 14.0 %all_to_all.30 = f32[16,8,128]{2,1,0:T(8,128)S(1)} all-to-all(f32[16,8,128]{2,1,0:T(8,128)S(1)} %broadcast_in_dim.20), channel_id=1, replica_groups=mesh['x'=4,'y'=4,'z_hi'=8,'z_mid'=2,'z_lo'=2,'core'=2] {'x','y'}, dimensions={0} | all-to-all | bytes 131072 | tf_op jit(solution)/shard_map/all_to_all | solution.py:38
  14.7 0.0 copy-done
  14.7 49.5 %all_to_all.31 = f32[16,8,128]{2,1,0:T(8,128)S(1)} all-to-all(f32[16,8,128]{2,1,0:T(8,128)S(1)} %broadcast_in_dim.21), channel_id=1, replica_groups=mesh['x'=4,'y'=4,'z_hi'=8,'z_mid'=2,'z_lo'=2,'core'=2] {'z_hi','z_mid'}, dimensions={0} | all-to-all | bytes 131072 | tf_op jit(solution)/shard_map/all_to_all | solution.py:38
  64.2 0.7 broadcast_in_dim.22
  64.9 0.0 copy-start.1
  64.9 0.0 copy-start.2
  64.9 7.1 %all-to-all-start.2 = ((f32[4,16,8,128]{3,2,1,0:T(8,128)}), f32[4,16,8,128]{3,2,1,0:T(8,128)S(1)}, u32[]{:S(2)}, u32[]{:S(2)}) async-start(f32[4,16,8,128]{3,2,1,0:T(8,128)} %broadcast_in_dim.22), calls=%async_computation.2 | async-start | bytes 524288 | tf_op jit(solution)/shard_map/all_to_all | solution.py:38
  72.7 0.0 copy-start.3
  72.7 0.6 copy-done.3
  73.3 0.0 copy-start.4
  73.3 0.7 fusion.32
  74.0 0.0 copy-done.4
  74.0 0.6 subtract_bitcast_fusion
  74.6 0.6 fusion.40
  75.3 0.0 copy-done.1
  75.3 0.0 copy-done.2
  75.3 1.1 fusion.11
  76.4 1.1 fusion.5
  77.5 1.1 fusion.17
  78.6 0.0 all-to-all-done.2
  78.6 0.9 convolution_bitcast_fusion
  79.5 0.1 reshape.32
  79.6 14.6 %all_to_all.32 = f32[64,2,384]{2,1,0:T(2,128)S(1)} all-to-all(f32[64,2,384]{2,1,0:T(2,128)S(1)} %reshape.32), channel_id=1, replica_groups=mesh['x'=4,'y'=4,'z_hi'=8,'z_mid'=2,'z_lo'=2,'core'=2] {'x','y','z_lo','..., dimensions={0} | all-to-all | bytes 393216 | tf_op jit(solution)/shard_map/all_to_all | solution.py:44
  94.2 0.1 reduce_sum.28
  94.4 24.8 %all_to_all.33 = f32[16,2,384]{2,1,0:T(2,128)S(1)} all-to-all(f32[16,2,384]{2,1,0:T(2,128)S(1)} %broadcast_in_dim.23), channel_id=1, replica_groups=mesh['x'=4,'y'=4,'z_hi'=8,'z_mid'=2,'z_lo'=2,'core'=2] {'z_hi','z_mid'}, dimensions={0} | all-to-all | bytes 98304 | tf_op jit(solution)/shard_map/all_to_all | solution.py:38
  119.1 0.1 broadcast_in_dim.24
  119.2 15.1 %all_to_all.34 = f32[64,2,384]{2,1,0:T(2,128)S(1)} all-to-all(f32[64,2,384]{2,1,0:T(2,128)S(1)} %broadcast_in_dim.24), channel_id=1, replica_groups=mesh['x'=4,'y'=4,'z_hi'=8,'z_mid'=2,'z_lo'=2,'core'=2] {'x','y','z_lo','..., dimensions={0} | all-to-all | bytes 393216 | tf_op jit(solution)/shard_map/all_to_all | solution.py:38
  134.3 0.8 reshape.33
  (4 shorter events, 0.1 us)
Async XLA Ops:
  0.7 14.0 %copy-start = (f32[1,8,128]{2,1,0:T(8,128)S(1)}, f32[1,8,128]{2,1,0:T(8,128)}, u32[]{:S(2)}) copy-start(f32[1,8,128]{2,1,0:T(8,128)} %param.9) | copy-start | bytes 12292
  64.9 10.4 %copy-start.1 = (f32[512,128]{1,0:T(8,128)S(1)}, f32[512,128]{1,0:T(8,128)}, u32[]{:S(2)}) copy-start(f32[512,128]{1,0:T(8,128)} %param.8) | copy-start | bytes 786436
  64.9 10.4 %copy-start.2 = (f32[512,128]{1,0:T(8,128)S(1)}, f32[512,128]{1,0:T(8,128)}, u32[]{:S(2)}) copy-start(f32[512,128]{1,0:T(8,128)} %param.7) | copy-start | bytes 786436
  64.9 13.7 %all-to-all-start.2 = ((f32[4,16,8,128]{3,2,1,0:T(8,128)}), f32[4,16,8,128]{3,2,1,0:T(8,128)S(1)}, u32[]{:S(2)}, u32[]{:S(2)}) async-start(f32[4,16,8,128]{3,2,1,0:T(8,128)} %broadcast_in_dim.22), calls=%async_computation.2 | async-start | bytes 524288 | tf_op jit(solution)/shard_map/all_to_all | solution.py:38
  72.7 0.7 copy-start.3
  73.3 0.7 copy-start.4

commit v2 on v1

--- a/solution.py
+++ b/solution.py
@@ -2,6 +2,7 @@
 import jax.numpy as jnp
 from jax import lax
 from jax.sharding import Mesh, PartitionSpec as P
+
 
 ROW = ("x", "y")
 COL = ("z_hi", "z_mid", "z_lo", "core")
@@ -53,14 +54,16 @@
     hits = (band_ids[:, None] == jnp.arange(table, dtype=jnp.int32)[None, :]).astype(jnp.float32)
     levels = jnp.sum(hits * band_energy[None, :], axis=1)
     shifts = eval_energy[None, :] - levels[:, None]
-    left_far = gather(mtx_left[0], ("z_hi", "z_mid"))
-    left_near = gather(left_far, ("z_lo", "core"))
-    left_rows = jnp.transpose(left_near, (1, 0, 2, 3)).reshape(-1, states)
+    left_rows = gather(mtx_left[0], COL[:-1]).reshape(-1, states)
     ratio = omega_sq / pole_freq
     shift_row = shifts[0]
     right_cols = gather(mtx_right[0], ROW).reshape(-1, states)
     product = kernel_rows(ratio, pole_freq, shift_row, right_cols, energies)
-    total = contract_rows(left_rows, product)
+    core = lax.axis_index("core")
+    halves = product.reshape(-1, 2, mtx_left.shape[1], energies * states)
+    other = lax.ppermute(lax.dynamic_index_in_dim(halves, 1 - core, 1, keepdims=False), "core", ((0, 1), (1, 0)))
+    half = lax.dynamic_index_in_dim(halves, core, 1, keepdims=False) + other
+    total = contract_rows(left_rows, half.reshape(-1, energies * states))
     return sum_everywhere(total, (*ROW, "z_lo", "core"), ("z_hi", "z_mid"))
 
 

time: 136 us -> 131 us (0.963)
  blocking collectives: 118 us -> 56.9 us
  starting transfers between devices: 7.13 us -> 40.3 us
  waiting for transfers between devices: 0.01 us -> 22.1 us
    all_to_all x4 -> x2, blocking collectives: 103 us -> 39.1 us  [gather(): lax.all_to_all(jnp.broadcast_to(block, (size, *block.shape)), axes, 0, 0)]
    all_to_all x1 -> x2, starting transfers between devices: 7.13 us -> 36 us  [gather(): lax.all_to_all(jnp.broadcast_to(block, (size, *block.shape)), axes, 0, 0)]
    all_to_all x1 -> x2, waiting for transfers between devices: 0.01 us -> 20.8 us  [gather(): lax.all_to_all(jnp.broadcast_to(block, (size, *block.shape)), axes, 0, 0)]
    ppermute x0 -> x1, starting transfers between devices: none -> 4.29 us  [shards(): lax.ppermute(lax.dynamic_index_in_dim(halves, 1 - core, 1, keepdims=False...]
    all_to_all x1, blocking collectives: 14.6 us -> 17.8 us  [sum_everywhere(): lax.all_to_all(total.reshape(size, rows // size, columns), near, 0, 0)]
  transfers between devices with their start and end apart: 1 -> 3, of which waited for: 0 -> 3; matrix products, arithmetic and copies ran while one was open for 4% -> 5% of each run, Pallas kernels for 0% -> 0%
where the time goes in v2:
time: 131 us
  blocking collectives  56.9 us (43%)
  starting transfers between devices  40.3 us (31%)
  waiting for transfers between devices  22.1 us (17%)
  matrix products  4.7 us (4%)
  local copies, waits for them, and re-layouts  4.57 us (3%)
  other arithmetic  1.42 us (1%)
    all_to_all x2, blocking collectives, gather(): lax.all_to_all(jnp.broadcast_to(block, (size, *block.shape)), axes, 0, 0)  39.1 us
    all_to_all x2, starting transfers between devices, gather(): lax.all_to_all(jnp.broadcast_to(block, (size, *block.shape)), axes, 0, 0)  36 us
    all_to_all x2, waiting for transfers between devices, gather(): lax.all_to_all(jnp.broadcast_to(block, (size, *block.shape)), axes, 0, 0)  20.8 us
    all_to_all x1, blocking collectives, sum_everywhere(): lax.all_to_all(total.reshape(size, rows // size, columns), near, 0, 0)  17.8 us
    ppermute x1, starting transfers between devices, shards(): lax.ppermute(lax.dynamic_index_in_dim(halves, 1 - core, 1, keepdims=False...  4.29 us
    dot_general x3, matrix products, kernel_rows(): jnp.dot(kern, right_cols, preferred_element_type=jnp.float32, precision=l...  4.24 us
  transfers between devices with their start and end apart: 3, of which 3 were waited for; matrix products, arithmetic and copies ran while one was open for 5% of the time, Pallas kernels for 0%

profile of v2, /device:TPU:1, one launch (start us, length us, event | category | flops | bytes accessed | tf_op | source)
XLA Modules:
  0.0 130.8 jit_solution(5463979109282336504)
XLA Ops:
  0.0 1.3 %broadcast_in_dim.8 = f32[16,8,128]{2,1,0:T(8,128)} broadcast(f32[8,128]{1,0:T(8,128)} %bitcast.29), dimensions={1,2} | broadcast | bytes 69632 | tf_op jit(solution)/shard_map/broadcast_in_dim | solution.py:39
  1.3 7.6 %all-to-all-start = ((f32[16,8,128]{2,1,0:T(8,128)}), f32[16,8,128]{2,1,0:T(8,128)S(1)}, u32[]{:S(2)}, u32[]{:S(2)}) async-start(f32[16,8,128]{2,1,0:T(8,128)} %broadcast_in_dim.8), calls=%async_computation | async-start | bytes 131072 | tf_op jit(solution)/shard_map/all_to_all | solution.py:39
  9.6 0.0 copy-start.4
  9.6 0.0 copy-start.3
  9.6 0.7 copy-done.3
  10.2 0.0 copy-start
  10.2 0.0 copy-start.1
  10.2 0.6 fusion.28
  10.9 0.0 copy-done.4
  10.9 0.6 subtract_bitcast_fusion
  11.5 0.6 fusion.36
  12.1 3.3 %all-to-all-done = f32[16,8,128]{2,1,0:T(8,128)S(1)} async-done(((f32[16,8,128]{2,1,0:T(8,128)}), f32[16,8,128]{2,1,0:T(8,128)S(1)}, u32[]{:S(2)}, u32[]{:S(2)}) %all-to-all-start) | async-done | bytes 65568 | tf_op jit(solution)/shard_map/all_to_all | solution.py:39
  15.4 0.0 copy-done
  15.4 0.7 broadcast_in_dim.18
  16.1 28.4 %all-to-all-start.1 = ((f32[32,8,128]{2,1,0:T(8,128)}), f32[32,8,128]{2,1,0:T(8,128)S(1)}, u32[]{:S(2)}, u32[]{:S(2)}) async-start(f32[32,8,128]{2,1,0:T(8,128)} %broadcast_in_dim.18), calls=%async_computation.1 | async-start | bytes 262144 | tf_op jit(solution)/shard_map/all_to_all | solution.py:39
  44.5 0.0 copy-done.1
  44.6 0.0 copy-start.2
  44.6 2.1 %fusion.1 = f32[512,128]{0,1:T(8,128)S(1)} fusion(f32[512,128]{1,0:T(8,128)S(1)} %copy-done.1, f32[]{:T(128)} %bitcast.6, f32[16,8,128]{2,1,0:T(8,128)S(1)} %all-to-all-done, f32[512,128]{1,0:T(8,128)} %param.7), kind=kOutput, calls=%fused_computation.5 | convolution fusion | flops 101056512 | bytes 851972 | tf_op jit(solution)/shard_map/dot_general | solution.py:27
  46.6 0.0 copy-done.2
  46.6 1.1 fusion.13
  47.7 1.1 fusion.7
  48.8 0.1 pad_maximum_fusion
  48.9 0.3 copy.15
  49.2 4.3 %collective-permute-start = (f32[32,8,384]{2,1,0:T(8,128)S(1)}, f32[32,8,384]{2,1,0:T(8,128)S(1)}, u32[]{:S(2)}, u32[]{:S(2)}) collective-permute-start(f32[32,8,384]{2,1,0:T(8,128)S(1)} %dynamic-slice_bitcast_fusion), channel_id=1, source_target_pairs={{0,1},{1,0},{2,3},{3,2},{4,5},{5,4},{6,7},{7,6},{8,9},{9,8},{10,11... | collective-permute-start | bytes 1179656 | tf_op jit(solution)/shard_map/ppermute | solution.py:64
  53.5 1.3 %collective-permute-done = f32[32,8,384]{2,1,0:T(8,128)S(1)} collective-permute-done((f32[32,8,384]{2,1,0:T(8,128)S(1)}, f32[32,8,384]{2,1,0:T(8,128)S(1)}, u32[]{:S(2)}, u32[]{:S(2)}) %collective-permute-start) | collective-permute-done | bytes 393248 | tf_op jit(solution)/shard_map/ppermute | solution.py:64
  54.8 17.4 %all-to-all-done.1 = f32[32,8,128]{2,1,0:T(8,128)S(1)} async-done(((f32[32,8,128]{2,1,0:T(8,128)}), f32[32,8,128]{2,1,0:T(8,128)S(1)}, u32[]{:S(2)}, u32[]{:S(2)}) %all-to-all-start.1) | async-done | bytes 131104 | tf_op jit(solution)/shard_map/all_to_all | solution.py:39
  72.3 0.5 convolution_bitcast_fusion
  72.7 0.1 reshape.34
  72.9 17.8 %all_to_all.25 = f32[64,2,384]{2,1,0:T(2,128)S(1)} all-to-all(f32[64,2,384]{2,1,0:T(2,128)S(1)} %reshape.34), channel_id=1, replica_groups=mesh['x'=4,'y'=4,'z_hi'=8,'z_mid'=2,'z_lo'=2,'core'=2] {'x','y','z_lo','..., dimensions={0} | all-to-all | bytes 393216 | tf_op jit(solution)/shard_map/all_to_all | solution.py:45
  90.6 0.1 reduce_sum.28
  90.8 23.7 %all_to_all.26 = f32[16,2,384]{2,1,0:T(2,128)S(1)} all-to-all(f32[16,2,384]{2,1,0:T(2,128)S(1)} %broadcast_in_dim.19), channel_id=1, replica_groups=mesh['x'=4,'y'=4,'z_hi'=8,'z_mid'=2,'z_lo'=2,'core'=2] {'z_hi','z_mid'}, dimensions={0} | all-to-all | bytes 98304 | tf_op jit(solution)/shard_map/all_to_all | solution.py:39
  114.5 0.1 broadcast_in_dim.20
  114.6 15.4 %all_to_all.27 = f32[64,2,384]{2,1,0:T(2,128)S(1)} all-to-all(f32[64,2,384]{2,1,0:T(2,128)S(1)} %broadcast_in_dim.20), channel_id=1, replica_groups=mesh['x'=4,'y'=4,'z_hi'=8,'z_mid'=2,'z_lo'=2,'core'=2] {'x','y','z_lo','..., dimensions={0} | all-to-all | bytes 393216 | tf_op jit(solution)/shard_map/all_to_all | solution.py:39
  130.0 0.8 reshape.35
  (3 shorter events, 0.1 us)
Async XLA Ops:
  1.3 14.1 %all-to-all-start = ((f32[16,8,128]{2,1,0:T(8,128)}), f32[16,8,128]{2,1,0:T(8,128)S(1)}, u32[]{:S(2)}, u32[]{:S(2)}) async-start(f32[16,8,128]{2,1,0:T(8,128)} %broadcast_in_dim.8), calls=%async_computation | async-start | bytes 131072 | tf_op jit(solution)/shard_map/all_to_all | solution.py:39
  9.6 1.3 %copy-start.4 = (f32[3]{0:T(128)S(1)}, f32[3]{0:T(128)}, u32[]{:S(2)}) copy-start(f32[3]{0:T(128)} %param.13) | copy-start | bytes 40
  9.6 0.7 copy-start.3
  10.2 5.2 %copy-start = (f32[1,8,128]{2,1,0:T(8,128)S(1)}, f32[1,8,128]{2,1,0:T(8,128)}, u32[]{:S(2)}) copy-start(f32[1,8,128]{2,1,0:T(8,128)} %param.9) | copy-start | bytes 12292
  10.2 34.3 %copy-start.1 = (f32[512,128]{1,0:T(8,128)S(1)}, f32[512,128]{1,0:T(8,128)}, u32[]{:S(2)}) copy-start(f32[512,128]{1,0:T(8,128)} %param.8) | copy-start | bytes 786436
  16.1 56.2 %all-to-all-start.1 = ((f32[32,8,128]{2,1,0:T(8,128)}), f32[32,8,128]{2,1,0:T(8,128)S(1)}, u32[]{:S(2)}, u32[]{:S(2)}) async-start(f32[32,8,128]{2,1,0:T(8,128)} %broadcast_in_dim.18), calls=%async_computation.1 | async-start | bytes 262144 | tf_op jit(solution)/shard_map/all_to_all | solution.py:39
  44.6 2.1 %copy-start.2 = (f32[512,128]{1,0:T(8,128)S(1)}, f32[512,128]{1,0:T(8,128)}, u32[]{:S(2)}) copy-start(f32[512,128]{1,0:T(8,128)} %param.7) | copy-start | bytes 786436
  49.2 5.6 %collective-permute-start = (f32[32,8,384]{2,1,0:T(8,128)S(1)}, f32[32,8,384]{2,1,0:T(8,128)S(1)}, u32[]{:S(2)}, u32[]{:S(2)}) collective-permute-start(f32[32,8,384]{2,1,0:T(8,128)S(1)} %dynamic-slice_bitcast_fusion), channel_id=1, source_target_pairs={{0,1},{1,0},{2,3},{3,2},{4,5},{5,4},{6,7},{7,6},{8,9},{9,8},{10,11... | collective-permute-start | bytes 1179656 | tf_op jit(solution)/shard_map/ppermute | solution.py:64

commit v3 on v1

v3 whole, which is shorter than its diff:
```python
import functools

import jax
import jax.numpy as jnp
from jax import lax
from jax.experimental import pallas as pl
from jax.experimental.pallas import tpu as pltpu
from jax.sharding import Mesh, PartitionSpec as P


ROW = ("x", "y")
COL = ("z_far", "z_lo", "core")
NEAR = (*ROW, "z_lo", "core")


def contract_rows(left, right):
    return lax.dot_general(
        left,
        right,
        (((0,), (0,)), ((), ())),
        precision=lax.Precision.HIGHEST,
        preferred_element_type=jnp.float32,
    )


def product_body(which_ref, shift_ref, omega_ref, freq_ref, right_ref, out_ref):
    which = which_ref[0]
    depth = freq_ref.shape[-1]
    states = right_ref.shape[1]
    freq = freq_ref[:, which].reshape(-1, depth)
    ratio = omega_ref[:, which].reshape(-1, depth) / freq
    for energy in range(shift_ref.shape[0]):
        gap = shift_ref[energy, 0:1, :] - freq
        kern = ratio * gap / (gap * gap + 0.09)
        out_ref[:, energy * states : (energy + 1) * states] = jnp.dot(
            kern,
            right_ref[...],
            preferred_element_type=jnp.float32,
            precision=lax.Precision.HIGHEST,
        )


def product_half(which, shifts, omega, freq, right_cols):
    chips, _, rows, depth = omega.shape
    energies = shifts.shape[0]
    states = right_cols.shape[1]
    vmem = pl.BlockSpec(memory_space=pltpu.VMEM)
    return pl.pallas_call(
        product_body,
        name="product_half",
        out_shape=jax.ShapeDtypeStruct((chips * rows, energies * states), jnp.float32),
        in_specs=[pl.BlockSpec(memory_space=pltpu.SMEM), vmem, vmem, vmem, vmem],
        out_specs=vmem,
        compiler_params=pltpu.CompilerParams(vmem_limit_bytes=8 << 20),
        cost_estimate=pl.CostEstimate(
            flops=2 * chips * rows * depth * states * energies,
            bytes_accessed=4 * (2 * omega.size + chips * rows * energies * states),
            transcendentals=0,
        ),
    )(jnp.reshape(which, (1,)), shifts, omega, freq, right_cols)


def gather(block, axes):
    size = lax.axis_size(axes)
    return lax.all_to_all(jnp.broadcast_to(block, (size, *block.shape)), axes, 0, 0)


def add_swapped(mine, theirs, axis):
    return mine + lax.ppermute(theirs, axis, ((0, 1), (1, 0)))


def sum_everywhere(total, near, far):
    rows, columns = total.shape
    size = lax.axis_size(near)
    pieces = lax.all_to_all(total.reshape(size, rows // size, columns), near, 0, 0)
    piece = jnp.sum(gather(jnp.sum(pieces, axis=0), far), axis=0)
    return gather(piece, near).reshape(rows, columns)


def shards(omega_sq, pole_freq, mtx_left, mtx_right, band_ids, band_energy, eval_energy):
    table = band_energy.shape[0]
    energies = eval_energy.shape[0]
    rows, states = mtx_left.shape[1:]
    depth = pole_freq.shape[1]
    hits = (band_ids[:, None] == jnp.arange(table, dtype=jnp.int32)[None, :]).astype(jnp.float32)
    levels = jnp.sum(hits * band_energy[None, :], axis=1)
    shifts = eval_energy[None, :] - levels[:, None]
    shift_rows = jnp.broadcast_to(shifts[0][:, None, None], (energies, 8, depth))
    core = lax.axis_index("core")
    z_lo = lax.axis_index("z_lo")
    blocks = (-1, 2, rows, depth)
    omega, freq = omega_sq.reshape(blocks), pole_freq.reshape(blocks)
    left_rows = gather(mtx_left[0], "z_far").reshape(-1, states)
    right_cols = gather(mtx_right[0], ROW).reshape(-1, states)
    half = functools.partial(
        product_half, shifts=shift_rows, omega=omega, freq=freq, right_cols=right_cols
    )
    theirs = half(1 - core)
    mine = half(core)
    mine = add_swapped(mine, theirs, "core")
    quarters = mine.reshape(-1, 2, rows, energies * states)
    quarter = functools.partial(lax.dynamic_index_in_dim, quarters, axis=1, keepdims=False)
    product = add_swapped(quarter(z_lo), quarter(1 - z_lo), "z_lo")
    total = contract_rows(left_rows, product.reshape(-1, energies * states))
    return sum_everywhere(total, NEAR, "z_far")


def solution(mesh):
    split = Mesh(mesh.devices.reshape(4, 4, 16, 2, 2), (*ROW, *COL))
    return jax.shard_map(
        shards,
        mesh=split,
        in_specs=(
            P(ROW, COL),
            P(ROW, COL),
            P(None, (*ROW, *COL), None),
            P(None, (*COL, *ROW), None),
            P(),
            P(),
            P(),
        ),
        out_specs=P(),
        check_vma=False,
    )
```

time: 136 us -> 135 us (level)
  blocking collectives: 118 us -> 60.9 us
  starting transfers between devices: 7.13 us -> 42.4 us
  waiting for transfers between devices: 0.01 us -> 22.1 us
  matrix products: 4.18 us -> 0.36 us
  local copies, waits for them, and re-layouts: 3.73 us -> 5.66 us
    all_to_all x4 -> x2, blocking collectives: 103 us -> 45.1 us  [gather(): lax.all_to_all(jnp.broadcast_to(block, (size, *block.shape)), axes, 0, 0)]
    all_to_all x1 -> x2, waiting for transfers between devices: 0.01 us -> 22.1 us  [gather(): lax.all_to_all(jnp.broadcast_to(block, (size, *block.shape)), axes, 0, 0)]
    all_to_all x1 -> x2, starting transfers between devices: 7.13 us -> 26.7 us  [gather(): lax.all_to_all(jnp.broadcast_to(block, (size, *block.shape)), axes, 0, 0)]
    ppermute x0 -> x2, starting transfers between devices: none -> 15.7 us  [add_swapped(): return mine + lax.ppermute(theirs, axis, ((0, 1), (1, 0)))]
    dot_general x3 -> x0, matrix products: 3.29 us -> none  [kernel_rows(): jnp.dot(kern, right_cols, preferred_element_type=jnp.float32, precision=l...]
    unnamed x10 -> x14, local copies, waits for them, and re-layouts: 0.67 us -> 2.57 us
  transfers between devices with their start and end apart: 1 -> 4, of which waited for: 0 -> 2; matrix products, arithmetic and copies ran while one was open for 4% -> 2% of each run, Pallas kernels for 0% -> 0%
where the time goes in v3:
time: 135 us
  blocking collectives  60.9 us (45%)
  starting transfers between devices  42.4 us (31%)
  waiting for transfers between devices  22.1 us (16%)
  local copies, waits for them, and re-layouts  5.66 us (4%)
  other arithmetic  1.55 us (1%)
    all_to_all x2, blocking collectives, gather(): lax.all_to_all(jnp.broadcast_to(block, (size, *block.shape)), axes, 0, 0)  45.1 us
    all_to_all x2, starting transfers between devices, gather(): lax.all_to_all(jnp.broadcast_to(block, (size, *block.shape)), axes, 0, 0)  26.7 us
    all_to_all x2, waiting for transfers between devices, gather(): lax.all_to_all(jnp.broadcast_to(block, (size, *block.shape)), axes, 0, 0)  22.1 us
    all_to_all x1, blocking collectives, sum_everywhere(): lax.all_to_all(total.reshape(size, rows // size, columns), near, 0, 0)  15.8 us
    ppermute x2, starting transfers between devices, add_swapped(): return mine + lax.ppermute(theirs, axis, ((0, 1), (1, 0)))  15.7 us
  transfers between devices with their start and end apart: 4, of which 2 were waited for; matrix products, arithmetic and copies ran while one was open for 2% of the time, Pallas kernels for 0%

profile of v3, /device:TPU:1, one launch (start us, length us, event | category | flops | bytes accessed | tf_op | source)
XLA Modules:
  0.0 134.8 jit_solution(16784541164959495510)
XLA Ops:
  0.0 1.3 broadcast_in_dim.11
  1.3 7.6 %all-to-all-start = ((f32[16,8,128]{2,1,0:T(8,128)}), f32[16,8,128]{2,1,0:T(8,128)S(1)}, u32[]{:S(2)}, u32[]{:S(2)}) async-start(f32[16,8,128]{2,1,0:T(8,128)} %broadcast_in_dim.11), calls=%async_computation | async-start | bytes 131072 | tf_op jit(solution)/shard_map/all_to_all | solution.py:65
  9.5 0.0 copy-start.5
  9.6 0.6 copy-done.5
  10.2 0.0 copy-start.6
  10.2 0.7 fusion.2
  10.9 0.0 copy-done.6
  10.9 0.7 broadcast_subtract_fusion
  11.6 3.8 %all-to-all-done = f32[16,8,128]{2,1,0:T(8,128)S(1)} async-done(((f32[16,8,128]{2,1,0:T(8,128)}), f32[16,8,128]{2,1,0:T(8,128)S(1)}, u32[]{:S(2)}, u32[]{:S(2)}) %all-to-all-start) | async-done | bytes 65568 | tf_op jit(solution)/shard_map/all_to_all | solution.py:65
  15.4 0.1 broadcast_in_dim.10.shift_ref
  15.5 0.0 copy-start
  15.5 0.9 copy-done
  16.4 0.0 copy-start.2
  16.4 0.9 copy-done.2
  17.4 0.0 copy-start.4
  17.4 0.0 copy-start.1
  17.4 0.0 copy-start.3
  17.4 0.5 product_half.3
  17.9 13.0 %collective-permute-start = (f32[256,384]{1,0:T(8,128)S(1)}, f32[256,384]{1,0:T(8,128)S(1)}, u32[]{:S(2)}, u32[]{:S(2)}) collective-permute-start(f32[256,384]{1,0:T(8,128)S(1)} %product_half.3), channel_id=1, source_target_pairs={{0,1},{1,0},{2,3},{3,2},{4,5},{5,4},{6,7},{7,6},{8,9},{9,8},{10,11... | collective-permute-start | bytes 1179656 | tf_op jit(solution)/shard_map/ppermute | solution.py:69
  30.9 0.0 copy-done.4
  30.9 0.6 broadcast_in_dim.24
  31.6 19.1 %all-to-all-start.1 = ((f32[16,8,128]{2,1,0:T(8,128)}), f32[16,8,128]{2,1,0:T(8,128)S(1)}, u32[]{:S(2)}, u32[]{:S(2)}) async-start(f32[16,8,128]{2,1,0:T(8,128)} %broadcast_in_dim.24), calls=%async_computation.1 | async-start | bytes 131072 | tf_op jit(solution)/shard_map/all_to_all | solution.py:65
  50.7 0.0 copy-done.1
  50.7 0.0 copy-done.3
  50.8 0.5 product_half.2
  51.3 0.0 collective-permute-done
  51.3 0.1 add.14
  51.4 2.6 %collective-permute-start.1 = (f32[16,8,384]{2,0,1:T(8,128)S(1)}, f32[16,8,384]{2,0,1:T(8,128)S(1)}, u32[]{:S(2)}, u32[]{:S(2)}) collective-permute-start(f32[16,8,384]{2,0,1:T(8,128)S(1)} %bitcast.27), channel_id=1, source_target_pairs={{0,2},{2,0},{1,3},{3,1},{4,6},{6,4},{5,7},{7,5},{8,10},{10,8},{9,1... | collective-permute-start | bytes 589832 | tf_op jit(solution)/shard_map/ppermute | solution.py:69
  54.1 18.3 %all-to-all-done.1 = f32[16,8,128]{2,1,0:T(8,128)S(1)} async-done(((f32[16,8,128]{2,1,0:T(8,128)}), f32[16,8,128]{2,1,0:T(8,128)S(1)}, u32[]{:S(2)}, u32[]{:S(2)}) %all-to-all-start.1) | async-done | bytes 65568 | tf_op jit(solution)/shard_map/all_to_all | solution.py:65
  72.3 0.0 collective-permute-done.1
  72.3 0.4 convolution_bitcast_fusion
  72.7 0.1 reshape.46
  72.8 15.8 %all_to_all.25 = f32[64,2,384]{2,1,0:T(2,128)S(1)} all-to-all(f32[64,2,384]{2,1,0:T(2,128)S(1)} %reshape.46), channel_id=1, replica_groups=mesh['x'=4,'y'=4,'z_far'=16,'z_lo'=2,'core'=2] {'x','y','z_lo','core'}, dimensions={0} | all-to-all | bytes 393216 | tf_op jit(solution)/shard_map/all_to_all | solution.py:75
  88.6 0.1 reduce_sum.28
  88.7 30.0 %all_to_all.26 = f32[16,2,384]{2,1,0:T(2,128)S(1)} all-to-all(f32[16,2,384]{2,1,0:T(2,128)S(1)} %broadcast_in_dim.25), channel_id=1, replica_groups=mesh['x'=4,'y'=4,'z_far'=16,'z_lo'=2,'core'=2] {'z_far'}, dimensions={0} | all-to-all | bytes 98304 | tf_op jit(solution)/shard_map/all_to_all | solution.py:65
  118.8 0.1 broadcast_in_dim.26
  118.8 15.1 %all_to_all.27 = f32[64,2,384]{2,1,0:T(2,128)S(1)} all-to-all(f32[64,2,384]{2,1,0:T(2,128)S(1)} %broadcast_in_dim.26), channel_id=1, replica_groups=mesh['x'=4,'y'=4,'z_far'=16,'z_lo'=2,'core'=2] {'x','y','z_lo','core'}, dimensions={0} | all-to-all | bytes 393216 | tf_op jit(solution)/shard_map/all_to_all | solution.py:65
  133.9 0.8 reshape.47
  (4 shorter events, 0.1 us)
Async XLA Ops:
  1.3 14.1 %all-to-all-start = ((f32[16,8,128]{2,1,0:T(8,128)}), f32[16,8,128]{2,1,0:T(8,128)S(1)}, u32[]{:S(2)}, u32[]{:S(2)}) async-start(f32[16,8,128]{2,1,0:T(8,128)} %broadcast_in_dim.11), calls=%async_computation | async-start | bytes 131072 | tf_op jit(solution)/shard_map/all_to_all | solution.py:65
  9.5 0.7 copy-start.5
  10.2 0.7 copy-start.6
  15.5 1.0 copy-start
  16.4 0.9 copy-start.2
  17.4 13.5 %copy-start.4 = (f32[1,8,128]{2,1,0:T(8,128)S(1)}, f32[1,8,128]{2,1,0:T(8,128)}, u32[]{:S(2)}) copy-start(f32[1,8,128]{2,1,0:T(8,128)} %param.9) | copy-start | bytes 12292
  17.4 33.3 %copy-start.1 = (f32[512,128]{1,0:T(8,128)S(1)}, f32[512,128]{1,0:T(8,128)}, u32[]{:S(2)}) copy-start(f32[512,128]{1,0:T(8,128)} %param.7) | copy-start | bytes 786436
  17.4 33.4 %copy-start.3 = (f32[512,128]{1,0:T(8,128)S(1)}, f32[512,128]{1,0:T(8,128)}, u32[]{:S(2)}) copy-start(f32[512,128]{1,0:T(8,128)} %param.8) | copy-start | bytes 786436
  17.9 33.4 %collective-permute-start = (f32[256,384]{1,0:T(8,128)S(1)}, f32[256,384]{1,0:T(8,128)S(1)}, u32[]{:S(2)}, u32[]{:S(2)}) collective-permute-start(f32[256,384]{1,0:T(8,128)S(1)} %product_half.3), channel_id=1, source_target_pairs={{0,1},{1,0},{2,3},{3,2},{4,5},{5,4},{6,7},{7,6},{8,9},{9,8},{10,11... | collective-permute-start | bytes 1179656 | tf_op jit(solution)/shard_map/ppermute | solution.py:69
  31.6 40.7 %all-to-all-start.1 = ((f32[16,8,128]{2,1,0:T(8,128)}), f32[16,8,128]{2,1,0:T(8,128)S(1)}, u32[]{:S(2)}, u32[]{:S(2)}) async-start(f32[16,8,128]{2,1,0:T(8,128)} %broadcast_in_dim.24), calls=%async_computation.1 | async-start | bytes 131072 | tf_op jit(solution)/shard_map/all_to_all | solution.py:65
  51.4 20.9 %collective-permute-start.1 = (f32[16,8,384]{2,0,1:T(8,128)S(1)}, f32[16,8,384]{2,0,1:T(8,128)S(1)}, u32[]{:S(2)}, u32[]{:S(2)}) collective-permute-start(f32[16,8,384]{2,0,1:T(8,128)S(1)} %bitcast.27), channel_id=1, source_target_pairs={{0,2},{2,0},{1,3},{3,1},{4,6},{6,4},{5,7},{7,5},{8,10},{10,8},{9,1... | collective-permute-start | bytes 589832 | tf_op jit(solution)/shard_map/ppermute | solution.py:69

commit v4 on v2

--- a/solution.py
+++ b/solution.py
@@ -5,7 +5,12 @@
 
 
 ROW = ("x", "y")
-COL = ("z_hi", "z_mid", "z_lo", "core")
+COL = ("z_far", "z_lo", "core")
+NEAR = (*ROW, "z_lo", "core")
+ROW_FIRST = 2 * 4 + 2
+NEAR_FIRST = (ROW_FIRST * 2 + 1) * 2
+FAR_FIRST = 8
+Z_FIRST = 16
 
 
 def contract_rows(left, right):
@@ -34,17 +39,23 @@
     return jnp.concatenate(parts, axis=1)
 
 
-def gather(block, axes):
-    size = lax.axis_size(axes)
-    return lax.all_to_all(jnp.broadcast_to(block, (size, *block.shape)), axes, 0, 0)
+def exchange(pieces, axes, first):
+    size = pieces.shape[0]
+    order = [(first + i) % size for i in range(size)]
+    return lax.all_to_all(pieces, axes, 0, 0, axis_index_groups=[order])
 
 
-def sum_everywhere(total, near, far):
+def gather(block, axes, first):
+    size = lax.axis_size(axes)
+    return exchange(jnp.broadcast_to(block, (size, *block.shape)), axes, first)
+
+
+def sum_everywhere(total):
     rows, columns = total.shape
-    size = lax.axis_size(near)
-    pieces = lax.all_to_all(total.reshape(size, rows // size, columns), near, 0, 0)
-    piece = jnp.sum(gather(jnp.sum(pieces, axis=0), far), axis=0)
-    return gather(piece, near).reshape(rows, columns)
+    size = lax.axis_size(NEAR)
+    pieces = exchange(total.reshape(size, rows // size, columns), NEAR, NEAR_FIRST)
+    piece = jnp.sum(gather(jnp.sum(pieces, axis=0), "z_far", FAR_FIRST), axis=0)
+    return gather(piece, NEAR, NEAR_FIRST).reshape(rows, columns)
 
 
 def shards(omega_sq, pole_freq, mtx_left, mtx_right, band_ids, band_energy, eval_energy):
@@ -54,21 +65,25 @@
     hits = (band_ids[:, None] == jnp.arange(table, dtype=jnp.int32)[None, :]).astype(jnp.float32)
     levels = jnp.sum(hits * band_energy[None, :], axis=1)
     shifts = eval_energy[None, :] - levels[:, None]
-    left_rows = gather(mtx_left[0], COL[:-1]).reshape(-1, states)
+    left_blocks = gather(mtx_left[0], COL[:-1], Z_FIRST)
     ratio = omega_sq / pole_freq
     shift_row = shifts[0]
-    right_cols = gather(mtx_right[0], ROW).reshape(-1, states)
+    right_blocks = gather(mtx_right[0], ROW, ROW_FIRST)
+    right_cols = jnp.roll(right_blocks, ROW_FIRST, axis=0).reshape(-1, states)
     product = kernel_rows(ratio, pole_freq, shift_row, right_cols, energies)
     core = lax.axis_index("core")
     halves = product.reshape(-1, 2, mtx_left.shape[1], energies * states)
-    other = lax.ppermute(lax.dynamic_index_in_dim(halves, 1 - core, 1, keepdims=False), "core", ((0, 1), (1, 0)))
+    other = lax.ppermute(
+        lax.dynamic_index_in_dim(halves, 1 - core, 1, keepdims=False), "core", ((0, 1), (1, 0))
+    )
     half = lax.dynamic_index_in_dim(halves, core, 1, keepdims=False) + other
+    left_rows = jnp.roll(left_blocks, Z_FIRST, axis=0).reshape(-1, states)
     total = contract_rows(left_rows, half.reshape(-1, energies * states))
-    return sum_everywhere(total, (*ROW, "z_lo", "core"), ("z_hi", "z_mid"))
+    return sum_everywhere(total)
 
 
 def solution(mesh):
-    split = Mesh(mesh.devices.reshape(4, 4, 8, 2, 2, 2), (*ROW, *COL))
+    split = Mesh(mesh.devices.reshape(4, 4, 16, 2, 2), (*ROW, *COL))
     return jax.shard_map(
         shards,
         mesh=split,

time: 131 us -> 118 us (0.901)
  waiting for transfers between devices: 22.1 us -> 5.06 us
  starting transfers between devices: 40.3 us -> 48.3 us
  blocking collectives: 56.9 us -> 53.1 us
    all_to_all x2, waiting for transfers between devices: 20.8 us -> 5.05 us  [exchange(): return lax.all_to_all(pieces, axes, 0, 0, axis_index_groups=[order])]
    all_to_all x2, starting transfers between devices: 36 us -> 44.8 us  [exchange(): return lax.all_to_all(pieces, axes, 0, 0, axis_index_groups=[order])]
    all_to_all x3, blocking collectives: 56.9 us -> 53.1 us  [exchange(): return lax.all_to_all(pieces, axes, 0, 0, axis_index_groups=[order])]
    ppermute x1, waiting for transfers between devices: 1.33 us -> 0.01 us  [shards(): lax.ppermute(lax.dynamic_index_in_dim(halves, 1 - core, 1, keepdims=False...]
  transfers between devices with their start and end apart: 3 -> 3, of which waited for: 3 -> 1; matrix products, arithmetic and copies ran while one was open for 5% -> 5% of each run, Pallas kernels for 0% -> 0%
where the time goes in v4:
time: 118 us; the launch traced here: 117 us
  blocking collectives  53.1 us (45%)
  starting transfers between devices  48.3 us (41%)
  waiting for transfers between devices  5.06 us (4%)
  local copies, waits for them, and re-layouts  4.89 us (4%)
  matrix products  3.59 us (3%)
  other arithmetic  1.42 us (1%)
    all_to_all x3, blocking collectives, exchange(): return lax.all_to_all(pieces, axes, 0, 0, axis_index_groups=[order])  53.1 us
    all_to_all x2, starting transfers between devices, exchange(): return lax.all_to_all(pieces, axes, 0, 0, axis_index_groups=[order])  44.8 us
    all_to_all x2, waiting for transfers between devices, exchange(): return lax.all_to_all(pieces, axes, 0, 0, axis_index_groups=[order])  5.05 us
    ppermute x1, starting transfers between devices, shards(): lax.ppermute(lax.dynamic_index_in_dim(halves, 1 - core, 1, keepdims=False...  3.42 us
    dot_general x3, matrix products, kernel_rows(): jnp.dot(kern, right_cols, preferred_element_type=jnp.float32, precision=l...  3.17 us
  transfers between devices with their start and end apart: 3, of which 1 were waited for; matrix products, arithmetic and copies ran while one was open for 5% of the time, Pallas kernels for 0%

profile of v4, /device:TPU:1, one launch (start us, length us, event | category | flops | bytes accessed | tf_op | source)
XLA Modules:
  0.0 117.1 jit_solution(5459086668563847190)
XLA Ops:
  0.0 1.3 %broadcast_in_dim.18 = f32[16,8,128]{2,1,0:T(8,128)} broadcast(f32[8,128]{1,0:T(8,128)} %bitcast.33), dimensions={1,2} | broadcast | bytes 69632 | tf_op jit(solution)/shard_map/broadcast_in_dim | solution.py:50
  1.3 9.5 %all-to-all-start.1 = ((f32[16,8,128]{2,1,0:T(8,128)}), f32[16,8,128]{2,1,0:T(8,128)S(1)}, u32[]{:S(2)}, u32[]{:S(2)}) async-start(f32[16,8,128]{2,1,0:T(8,128)} %broadcast_in_dim.18), calls=%async_computation.1 | async-start | bytes 131072 | tf_op jit(solution)/shard_map/all_to_all | solution.py:45
  11.5 0.0 copy-start.3
  11.5 0.6 copy-done.3
  12.2 0.0 copy-start.4
  12.2 0.6 fusion.28
  12.8 0.0 copy-done.4
  12.8 0.6 subtract_bitcast_fusion
  13.4 0.0 copy-start
  13.4 0.6 fusion.40
  14.0 0.0 all-to-all-done.1
  14.0 0.1 copy-done
  14.1 0.0 copy-start.1
  14.1 0.0 copy-start.2
  14.1 0.7 broadcast_in_dim.8
  14.8 35.3 %all-to-all-start = ((f32[32,8,128]{2,1,0:T(8,128)}), f32[32,8,128]{2,1,0:T(8,128)S(1)}, u32[]{:S(2)}, u32[]{:S(2)}) async-start(f32[32,8,128]{2,1,0:T(8,128)} %broadcast_in_dim.8), calls=%async_computation | async-start | bytes 262144 | tf_op jit(solution)/shard_map/all_to_all | solution.py:45
  50.2 0.0 copy-done.1
  50.2 0.0 copy-done.2
  50.2 1.1 fusion.15
  51.2 1.0 fusion.9
  52.3 1.1 fusion.3
  53.4 0.1 pad_maximum_fusion
  53.4 0.3 copy.23
  53.7 3.4 %collective-permute-start = (f32[32,8,384]{2,1,0:T(8,128)S(1)}, f32[32,8,384]{2,1,0:T(8,128)S(1)}, u32[]{:S(2)}, u32[]{:S(2)}) collective-permute-start(f32[32,8,384]{2,1,0:T(8,128)S(1)} %dynamic-slice_bitcast_fusion), channel_id=1, source_target_pairs={{0,1},{1,0},{2,3},{3,2},{4,5},{5,4},{6,7},{7,6},{8,9},{9,8},{10,11... | collective-permute-start | bytes 1179656 | tf_op jit(solution)/shard_map/ppermute | solution.py:76
  57.2 5.1 %all-to-all-done = f32[32,8,128]{2,1,0:T(8,128)S(1)} async-done(((f32[32,8,128]{2,1,0:T(8,128)}), f32[32,8,128]{2,1,0:T(8,128)S(1)}, u32[]{:S(2)}, u32[]{:S(2)}) %all-to-all-start) | async-done | bytes 131104 | tf_op jit(solution)/shard_map/all_to_all | solution.py:45
  62.2 0.1 copy.22
  62.3 0.1 dot_general.17
  62.4 0.0 collective-permute-done
  62.4 0.4 fusion
  62.9 0.2 copy.25
  63.0 12.8 %all_to_all.25 = f32[64,2,384]{2,1,0:T(2,128)S(1)} all-to-all(f32[64,2,384]{2,1,0:T(2,128)S(1)} %copy.25), channel_id=1, replica_groups={{642,643,704,705,706,707,768,769,770,771,832,833,834,835,896,897,898,89..., dimensions={0} | all-to-all | bytes 393216 | tf_op jit(solution)/shard_map/all_to_all | solution.py:45
  75.8 0.1 reduce_sum.28
  75.9 27.3 %all_to_all.26 = f32[16,2,384]{2,1,0:T(2,128)S(1)} all-to-all(f32[16,2,384]{2,1,0:T(2,128)S(1)} %broadcast_in_dim.19), channel_id=1, replica_groups={{32,36,40,44,48,52,56,60,0,4,8,12,16,20,24,28},{33,37,41,45,49,53,57,61..., dimensions={0} | all-to-all | bytes 98304 | tf_op jit(solution)/shard_map/all_to_all | solution.py:45
  103.3 0.1 broadcast_in_dim.20
  103.3 13.0 %all_to_all.27 = f32[64,2,384]{2,1,0:T(2,128)S(1)} all-to-all(f32[64,2,384]{2,1,0:T(2,128)S(1)} %broadcast_in_dim.20), channel_id=1, replica_groups={{642,643,704,705,706,707,768,769,770,771,832,833,834,835,896,897,898,89..., dimensions={0} | all-to-all | bytes 393216 | tf_op jit(solution)/shard_map/all_to_all | solution.py:45
  116.3 0.8 reshape.39
  (7 shorter events, 0.1 us)
Async XLA Ops:
  1.3 12.7 %all-to-all-start.1 = ((f32[16,8,128]{2,1,0:T(8,128)}), f32[16,8,128]{2,1,0:T(8,128)S(1)}, u32[]{:S(2)}, u32[]{:S(2)}) async-start(f32[16,8,128]{2,1,0:T(8,128)} %broadcast_in_dim.18), calls=%async_computation.1 | async-start | bytes 131072 | tf_op jit(solution)/shard_map/all_to_all | solution.py:45
  11.5 0.7 copy-start.3
  12.2 0.7 copy-start.4
  13.4 0.7 copy-start
  14.1 36.0 %copy-start.1 = (f32[512,128]{1,0:T(8,128)S(1)}, f32[512,128]{1,0:T(8,128)}, u32[]{:S(2)}) copy-start(f32[512,128]{1,0:T(8,128)} %param.8) | copy-start | bytes 786436
  14.1 36.0 %copy-start.2 = (f32[512,128]{1,0:T(8,128)S(1)}, f32[512,128]{1,0:T(8,128)}, u32[]{:S(2)}) copy-start(f32[512,128]{1,0:T(8,128)} %param.7) | copy-start | bytes 786436
  14.8 47.4 %all-to-all-start = ((f32[32,8,128]{2,1,0:T(8,128)}), f32[32,8,128]{2,1,0:T(8,128)S(1)}, u32[]{:S(2)}, u32[]{:S(2)}) async-start(f32[32,8,128]{2,1,0:T(8,128)} %broadcast_in_dim.8), calls=%async_computation | async-start | bytes 262144 | tf_op jit(solution)/shard_map/all_to_all | solution.py:45
  53.7 8.7 %collective-permute-start = (f32[32,8,384]{2,1,0:T(8,128)S(1)}, f32[32,8,384]{2,1,0:T(8,128)S(1)}, u32[]{:S(2)}, u32[]{:S(2)}) collective-permute-start(f32[32,8,384]{2,1,0:T(8,128)S(1)} %dynamic-slice_bitcast_fusion), channel_id=1, source_target_pairs={{0,1},{1,0},{2,3},{3,2},{4,5},{5,4},{6,7},{7,6},{8,9},{9,8},{10,11... | collective-permute-start | bytes 1179656 | tf_op jit(solution)/shard_map/ppermute | solution.py:76

commit v5 on v4

v5 whole, which is shorter than its diff:
```python
import jax
import jax.numpy as jnp
from jax import lax
from jax.experimental import pallas as pl
from jax.experimental.pallas import tpu as pltpu
from jax.sharding import Mesh, PartitionSpec as P


ROW = ("x", "y")
COL = ("z_far", "z_lo", "core")
NEAR = (*ROW, "z_lo", "core")
ROW_FIRST = 2 * 4 + 2
NEAR_FIRST = (ROW_FIRST * 2 + 1) * 2
FAR_FIRST = 8


def dot(left, right):
    return jnp.dot(
        left,
        right,
        precision=lax.Precision.HIGHEST,
        preferred_element_type=jnp.float32,
    )


def block_body(place_ref, shift_ref, omega_ref, freq_ref, mine_ref, other_ref, right_ref, out_ref, left_ref):
    z_lo, core = place_ref[0], place_ref[1]
    chips = left_ref.shape[0]
    states = right_ref.shape[1]
    for blocks, at_core in ((mine_ref, core), (other_ref, 1 - core)):
        for i, at_z in enumerate((z_lo, 1 - z_lo)):
            left_ref[:FAR_FIRST, at_z, at_core] = blocks[i, chips - FAR_FIRST :]
            left_ref[FAR_FIRST:, at_z, at_core] = blocks[i, : chips - FAR_FIRST]
    left = left_ref[...].reshape(-1, states).T
    freq = freq_ref[...]
    ratio = omega_ref[...] / freq
    for energy in range(shift_ref.shape[0]):
        gap = shift_ref[energy, 0:1, :] - freq
        kern = ratio * gap / (gap * gap + 0.09)
        out_ref[:, energy * states : (energy + 1) * states] = dot(dot(left, kern), right_ref[...])


def block_sum(place, shifts, omega, freq, mine, other, right_cols):
    rows, depth = freq.shape
    energies = shifts.shape[0]
    states = right_cols.shape[1]
    pair, chips, lines, _ = mine.shape
    vmem = pl.BlockSpec(memory_space=pltpu.VMEM)
    return pl.pallas_call(
        block_body,
        name="block_sum",
        out_shape=jax.ShapeDtypeStruct((states, energies * states), jnp.float32),
        in_specs=[pl.BlockSpec(memory_space=pltpu.SMEM)] + [vmem] * 6,
        out_specs=vmem,
        scratch_shapes=[pltpu.VMEM((chips, pair, 2, lines, states), jnp.float32)],
        compiler_params=pltpu.CompilerParams(vmem_limit_bytes=16 << 20),
        cost_estimate=pl.CostEstimate(
            flops=2 * (rows + depth) * depth * states * energies,
            bytes_accessed=4 * (3 * freq.size + energies * states * states),
            transcendentals=0,
        ),
    )(place, shifts, omega, freq, mine, other, right_cols)


def exchange(pieces, axes, first):
    size = pieces.shape[0]
    order = [(first + i) % size for i in range(size)]
    return lax.all_to_all(pieces, axes, 0, 0, axis_index_groups=[order])


def gather(block, axes, first):
    size = lax.axis_size(axes)
    return exchange(jnp.broadcast_to(block, (size, *block.shape)), axes, first)


def sum_everywhere(total):
    rows, columns = total.shape
    size = lax.axis_size(NEAR)
    pieces = exchange(total.reshape(size, rows // size, columns), NEAR, NEAR_FIRST)
    piece = jnp.sum(gather(jnp.sum(pieces, axis=0), "z_far", FAR_FIRST), axis=0)
    return gather(piece, NEAR, NEAR_FIRST).reshape(rows, columns)


def with_partner(blocks, axis):
    return jnp.stack([blocks, lax.ppermute(blocks, axis, ((0, 1), (1, 0)))])


def shards(omega_sq, pole_freq, mtx_left, mtx_right, band_ids, band_energy, eval_energy):
    table = band_energy.shape[0]
    energies = eval_energy.shape[0]
    states = mtx_left.shape[2]
    depth = pole_freq.shape[1]
    hits = (band_ids[:, None] == jnp.arange(table, dtype=jnp.int32)[None, :]).astype(jnp.float32)
    levels = jnp.sum(hits * band_energy[None, :], axis=1)
    shifts = eval_energy[None, :] - levels[:, None]
    shift_rows = jnp.broadcast_to(shifts[0][:, None, None], (energies, 8, depth))
    place = jnp.stack([lax.axis_index("z_lo"), lax.axis_index("core")])
    left_far = gather(mtx_left[0], "z_far", FAR_FIRST)
    mine = with_partner(left_far, "z_lo")
    other = lax.ppermute(mine, "core", ((0, 1), (1, 0)))
    right_blocks = gather(mtx_right[0], ROW, ROW_FIRST)
    right_cols = jnp.roll(right_blocks, ROW_FIRST, axis=0).reshape(-1, states)
    total = block_sum(place, shift_rows, omega_sq, pole_freq, mine, other, right_cols)
    return sum_everywhere(total)


def solution(mesh):
    split = Mesh(mesh.devices.reshape(4, 4, 16, 2, 2), (*ROW, *COL))
    return jax.shard_map(
        shards,
        mesh=split,
        in_specs=(
            P(ROW, COL),
            P(ROW, COL),
            P(None, (*ROW, *COL), None),
            P(None, (*COL, *ROW), None),
            P(),
            P(),
            P(),
        ),
        out_specs=P(),
        check_vma=False,
    )
```

time: 118 us -> 119 us (level)
  matrix products: 3.59 us -> 0 us
  waiting for transfers between devices: 5.06 us -> 8.57 us
  starting transfers between devices: 48.3 us -> 51.1 us
  Pallas kernels: 0 us -> 2 us
  local copies, waits for them, and re-layouts: 4.89 us -> 3.04 us
  blocking collectives: 53.1 us -> 51.3 us
    dot_general x4 -> x0, matrix products: 3.59 us -> none  [the longest x3 3.17 us: kernel_rows(): jnp.dot(kern, right_cols, preferred_element_type=jnp.float32, precision=l...]
    ppermute x1 -> x2, waiting for transfers between devices: 0.01 us -> 3.21 us  [the longest x1 2.36 us: with_partner(): return jnp.stack([blocks, lax.ppermute(blocks, axis, ((0, 1), (1, 0)))])]
    ppermute x1 -> x2, starting transfers between devices: 3.42 us -> 6.55 us  [the longest x1 4.55 us: shards(): other = lax.ppermute(mine, 'core', ((0, 1), (1, 0)))]
    pallas_call x0 -> x1, Pallas kernels: none -> 2 us  [block_sum(): pl.pallas_call(block_body, name='block_sum', out_shape=jax.ShapeDtypeStru...]
    all_to_all x3, blocking collectives: 53.1 us -> 51.3 us  [exchange(): return lax.all_to_all(pieces, axes, 0, 0, axis_index_groups=[order])]
  transfers between devices with their start and end apart: 3 -> 4, of which waited for: 1 -> 3; matrix products, arithmetic and copies ran while one was open for 5% -> 1% of each run, Pallas kernels for 0% -> 0%
where the time goes in v5:
time: 119 us; the launch traced here: 118 us
  blocking collectives  51.3 us (43%)
  starting transfers between devices  51.1 us (43%)
  waiting for transfers between devices  8.57 us (7%)
  local copies, waits for them, and re-layouts  3.04 us (3%)
  Pallas kernels  2 us (2%)
  other arithmetic  1.46 us (1%)
    all_to_all x3, blocking collectives, exchange(): return lax.all_to_all(pieces, axes, 0, 0, axis_index_groups=[order])  51.3 us
    all_to_all x2, starting transfers between devices, exchange(): return lax.all_to_all(pieces, axes, 0, 0, axis_index_groups=[order])  44.5 us
    all_to_all x2, waiting for transfers between devices, exchange(): return lax.all_to_all(pieces, axes, 0, 0, axis_index_groups=[order])  5.36 us
    ppermute x1, starting transfers between devices, shards(): other = lax.ppermute(mine, 'core', ((0, 1), (1, 0)))  4.55 us
  transfers between devices with their start and end apart: 4, of which 3 were waited for; matrix products, arithmetic and copies ran while one was open for 1% of the time, Pallas kernels for 0%

profile of v5, /device:TPU:1, one launch (start us, length us, event | category | flops | bytes accessed | tf_op | source)
XLA Modules:
  0.0 118.2 jit_solution(8244288481066872148)
XLA Ops:
  0.0 1.3 %broadcast_in_dim.11 = f32[16,8,128]{2,1,0:T(8,128)} broadcast(f32[8,128]{1,0:T(8,128)} %bitcast.12), dimensions={1,2} | broadcast | bytes 69632 | tf_op jit(solution)/shard_map/broadcast_in_dim | solution.py:73
  1.3 0.0 copy-start.3
  1.3 35.7 %all-to-all-start = ((f32[16,8,128]{2,1,0:T(8,128)}), f32[16,8,128]{2,1,0:T(8,128)S(1)}, u32[]{:S(2)}, u32[]{:S(2)}) async-start(f32[16,8,128]{2,1,0:T(8,128)} %broadcast_in_dim.11), calls=%async_computation | async-start | bytes 131072 | tf_op jit(solution)/shard_map/all_to_all | solution.py:68
  37.0 0.0 copy-start.2
  37.7 0.0 copy-done.3
  37.7 0.6 fusion
  38.3 5.4 %all-to-all-done = f32[16,8,128]{2,1,0:T(8,128)S(1)} async-done(((f32[16,8,128]{2,1,0:T(8,128)}), f32[16,8,128]{2,1,0:T(8,128)S(1)}, u32[]{:S(2)}, u32[]{:S(2)}) %all-to-all-start) | async-done | bytes 65568 | tf_op jit(solution)/shard_map/all_to_all | solution.py:68
  43.7 0.0 copy-done.2
  43.7 0.6 broadcast_in_dim.24
  44.3 0.0 copy-start.4
  44.3 8.8 %all-to-all-start.1 = ((f32[16,8,128]{2,1,0:T(8,128)}), f32[16,8,128]{2,1,0:T(8,128)S(1)}, u32[]{:S(2)}, u32[]{:S(2)}) async-start(f32[16,8,128]{2,1,0:T(8,128)} %broadcast_in_dim.24), calls=%async_computation.1 | async-start | bytes 131072 | tf_op jit(solution)/shard_map/all_to_all | solution.py:68
  53.1 2.0 %collective-permute-start = (f32[16,8,128]{2,1,0:T(8,128)S(1)}, f32[16,8,128]{2,1,0:T(8,128)S(1)}, u32[]{:S(2)}, u32[]{:S(2)}) collective-permute-start(f32[16,8,128]{2,1,0:T(8,128)S(1)} %all-to-all-done), channel_id=1, source_target_pairs={{0,2},{2,0},{1,3},{3,1},{4,6},{6,4},{5,7},{7,5},{8,10},{10,8},{9,1... | collective-permute-start | bytes 196616 | tf_op jit(solution)/shard_map/ppermute | solution.py:85
  55.1 0.0 copy-done.4
  55.2 0.6 broadcast_subtract_fusion
  55.8 2.4 %collective-permute-done = f32[16,8,128]{2,1,0:T(8,128)S(1)} collective-permute-done((f32[16,8,128]{2,1,0:T(8,128)S(1)}, f32[16,8,128]{2,1,0:T(8,128)S(1)}, u32[]{:S(2)}, u32[]{:S(2)}) %collective-permute-start) | collective-permute-done | bytes 65568 | tf_op jit(solution)/shard_map/ppermute | solution.py:85
  58.1 0.0 copy-start
  58.1 0.0 copy-start.1
  58.1 4.5 %collective-permute-start.1 = (f32[2,16,8,128]{3,2,1,0:T(8,128)S(1)}, f32[2,16,8,128]{3,2,1,0:T(8,128)S(1)}, u32[]{:S(2)}, u32[]{:S(2)}) collective-permute-start(f32[2,16,8,128]{3,2,1,0:T(8,128)S(1)} %pad_maximum_fusion.mine_ref), channel_id=1, source_target_pairs={{0,1},{1,0},{2,3},{3,2},{4,5},{5,4},{6,7},{7,6},{8,9},{9,8},{10,11... | collective-permute-start | bytes 393224 | tf_op jit(solution)/shard_map/ppermute | solution.py:100
  62.7 0.1 pad_add_fusion.place_ref
  62.8 0.0 all-to-all-done.1
  62.8 0.9 collective-permute-done.1.other_ref
  63.7 0.1 broadcast_in_dim.10.shift_ref
  63.7 0.0 copy-done
  63.7 0.0 copy-done.1
  63.7 2.0 %block_sum.1 = f32[128,384]{1,0:T(8,128)S(1)} custom-call(s32[2]{0:T(128)S(1)} %pad_add_fusion.place_ref, f32[3,8,128]{2,1,0:T(8,128)S(1)} %broadcast_in_dim.10.shift_ref, f32[512,128]{1,0:T(8,128)S(1)} %copy-done, f32[512,128]{1,0:T(8,128)S(1)} %copy-done.1, f32[2,16,8,128]{3,2,1,0:T(8,128)S(1)} %pad_maximum_fusion.mine_ref, ...), custom_call_target="tpu_custom_call" | custom-call | flops 62914560 | bytes 983040 | tf_op jit(solution)/shard_map/block_sum/pallas_call | solution.py:49
  65.8 0.1 reshape.24
  65.9 12.0 %all_to_all.25 = f32[64,2,384]{2,1,0:T(2,128)S(1)} all-to-all(f32[64,2,384]{2,1,0:T(2,128)S(1)} %reshape.24), channel_id=1, replica_groups={{642,643,704,705,706,707,768,769,770,771,832,833,834,835,896,897,898,89..., dimensions={0} | all-to-all | bytes 393216 | tf_op jit(solution)/shard_map/all_to_all | solution.py:68
  77.9 0.1 reduce_sum.28
  78.0 26.5 %all_to_all.26 = f32[16,2,384]{2,1,0:T(2,128)S(1)} all-to-all(f32[16,2,384]{2,1,0:T(2,128)S(1)} %broadcast_in_dim.25), channel_id=1, replica_groups={{32,36,40,44,48,52,56,60,0,4,8,12,16,20,24,28},{33,37,41,45,49,53,57,61..., dimensions={0} | all-to-all | bytes 98304 | tf_op jit(solution)/shard_map/all_to_all | solution.py:68
  104.5 0.1 broadcast_in_dim.26
  104.6 12.9 %all_to_all.27 = f32[64,2,384]{2,1,0:T(2,128)S(1)} all-to-all(f32[64,2,384]{2,1,0:T(2,128)S(1)} %broadcast_in_dim.26), channel_id=1, replica_groups={{642,643,704,705,706,707,768,769,770,771,832,833,834,835,896,897,898,89..., dimensions={0} | all-to-all | bytes 393216 | tf_op jit(solution)/shard_map/all_to_all | solution.py:68
  117.4 0.8 reshape.25
  (6 shorter events, 0.1 us)
Async XLA Ops:
  1.3 36.3 %copy-start.3 = (f32[64]{0:T(128)S(1)}, f32[64]{0:T(128)}, u32[]{:S(2)}) copy-start(f32[64]{0:T(128)} %param.12) | copy-start | bytes 772
  1.3 42.3 %all-to-all-start = ((f32[16,8,128]{2,1,0:T(8,128)}), f32[16,8,128]{2,1,0:T(8,128)S(1)}, u32[]{:S(2)}, u32[]{:S(2)}) async-start(f32[16,8,128]{2,1,0:T(8,128)} %broadcast_in_dim.11), calls=%async_computation | async-start | bytes 131072 | tf_op jit(solution)/shard_map/all_to_all | solution.py:68
  37.0 6.7 %copy-start.2 = (f32[1,8,128]{2,1,0:T(8,128)S(1)}, f32[1,8,128]{2,1,0:T(8,128)}, u32[]{:S(2)}) copy-start(f32[1,8,128]{2,1,0:T(8,128)} %param.10) | copy-start | bytes 12292
  44.3 10.8 %copy-start.4 = (f32[3]{0:T(128)S(1)}, f32[3]{0:T(128)}, u32[]{:S(2)}) copy-start(f32[3]{0:T(128)} %param.13) | copy-start | bytes 40
  44.3 18.5 %all-to-all-start.1 = ((f32[16,8,128]{2,1,0:T(8,128)}), f32[16,8,128]{2,1,0:T(8,128)S(1)}, u32[]{:S(2)}, u32[]{:S(2)}) async-start(f32[16,8,128]{2,1,0:T(8,128)} %broadcast_in_dim.24), calls=%async_computation.1 | async-start | bytes 131072 | tf_op jit(solution)/shard_map/all_to_all | solution.py:68
  53.1 5.0 %collective-permute-start = (f32[16,8,128]{2,1,0:T(8,128)S(1)}, f32[16,8,128]{2,1,0:T(8,128)S(1)}, u32[]{:S(2)}, u32[]{:S(2)}) collective-permute-start(f32[16,8,128]{2,1,0:T(8,128)S(1)} %all-to-all-done), channel_id=1, source_target_pairs={{0,2},{2,0},{1,3},{3,1},{4,6},{6,4},{5,7},{7,5},{8,10},{10,8},{9,1... | collective-permute-start | bytes 196616 | tf_op jit(solution)/shard_map/ppermute | solution.py:85
  58.1 5.6 %copy-start = (f32[512,128]{1,0:T(8,128)S(1)}, f32[512,128]{1,0:T(8,128)}, u32[]{:S(2)}) copy-start(f32[512,128]{1,0:T(8,128)} %omega_ref.1) | copy-start | bytes 786436
  58.1 5.6 %copy-start.1 = (f32[512,128]{1,0:T(8,128)S(1)}, f32[512,128]{1,0:T(8,128)}, u32[]{:S(2)}) copy-start(f32[512,128]{1,0:T(8,128)} %freq_ref.1) | copy-start | bytes 786436
  58.1 5.5 %collective-permute-start.1 = (f32[2,16,8,128]{3,2,1,0:T(8,128)S(1)}, f32[2,16,8,128]{3,2,1,0:T(8,128)S(1)}, u32[]{:S(2)}, u32[]{:S(2)}) collective-permute-start(f32[2,16,8,128]{3,2,1,0:T(8,128)S(1)} %pad_maximum_fusion.mine_ref), channel_id=1, source_target_pairs={{0,1},{1,0},{2,3},{3,2},{4,5},{5,4},{6,7},{7,6},{8,9},{9,8},{10,11... | collective-permute-start | bytes 393224 | tf_op jit(solution)/shard_map/ppermute | solution.py:100

commit v6 on v5

--- a/solution.py
+++ b/solution.py
@@ -23,43 +23,52 @@
     )
 
 
-def block_body(place_ref, shift_ref, omega_ref, freq_ref, mine_ref, other_ref, right_ref, out_ref, left_ref):
-    z_lo, core = place_ref[0], place_ref[1]
+def half_terms(z_lo, core, shift_ref, omega_ref, freq_ref, blocks_ref, left_ref):
     chips = left_ref.shape[0]
-    states = right_ref.shape[1]
-    for blocks, at_core in ((mine_ref, core), (other_ref, 1 - core)):
-        for i, at_z in enumerate((z_lo, 1 - z_lo)):
-            left_ref[:FAR_FIRST, at_z, at_core] = blocks[i, chips - FAR_FIRST :]
-            left_ref[FAR_FIRST:, at_z, at_core] = blocks[i, : chips - FAR_FIRST]
-    left = left_ref[...].reshape(-1, states).T
-    freq = freq_ref[...]
-    ratio = omega_ref[...] / freq
+    depth = freq_ref.shape[-1]
+    for i, at_z in enumerate((z_lo, 1 - z_lo)):
+        left_ref[:FAR_FIRST, at_z] = blocks_ref[i, chips - FAR_FIRST :]
+        left_ref[FAR_FIRST:, at_z] = blocks_ref[i, : chips - FAR_FIRST]
+    left = left_ref[...].reshape(-1, left_ref.shape[-1]).T
+    freq = freq_ref[:, core].reshape(-1, depth)
+    ratio = omega_ref[:, core].reshape(-1, depth) / freq
     for energy in range(shift_ref.shape[0]):
         gap = shift_ref[energy, 0:1, :] - freq
-        kern = ratio * gap / (gap * gap + 0.09)
-        out_ref[:, energy * states : (energy + 1) * states] = dot(dot(left, kern), right_ref[...])
+        yield dot(left, ratio * gap / (gap * gap + 0.09))
 
 
-def block_sum(place, shifts, omega, freq, mine, other, right_cols):
-    rows, depth = freq.shape
+def mine_body(place_ref, shift_ref, omega_ref, freq_ref, mine_ref, out_ref, left_ref):
+    z_lo, core = place_ref[0], place_ref[1]
+    terms = half_terms(z_lo, core, shift_ref, omega_ref, freq_ref, mine_ref, left_ref)
+    for energy, term in enumerate(terms):
+        out_ref[energy] = term
+
+
+def rest_body(place_ref, shift_ref, omega_ref, freq_ref, other_ref, part_ref, right_ref, out_ref, left_ref):
+    z_lo, core = place_ref[0], place_ref[1]
+    states = right_ref.shape[1]
+    terms = half_terms(z_lo, 1 - core, shift_ref, omega_ref, freq_ref, other_ref, left_ref)
+    for energy, term in enumerate(terms):
+        out_ref[:, energy * states : (energy + 1) * states] = dot(part_ref[energy] + term, right_ref[...])
+
+
+def local_kernel(body, out_shape, place, shifts, omega, freq, blocks, *more):
+    lines, depth = blocks.shape[2:]
     energies = shifts.shape[0]
-    states = right_cols.shape[1]
-    pair, chips, lines, _ = mine.shape
     vmem = pl.BlockSpec(memory_space=pltpu.VMEM)
     return pl.pallas_call(
-        block_body,
-        name="block_sum",
-        out_shape=jax.ShapeDtypeStruct((states, energies * states), jnp.float32),
-        in_specs=[pl.BlockSpec(memory_space=pltpu.SMEM)] + [vmem] * 6,
+        body,
+        out_shape=jax.ShapeDtypeStruct(out_shape, jnp.float32),
+        in_specs=[pl.BlockSpec(memory_space=pltpu.SMEM)] + [vmem] * (4 + len(more)),
         out_specs=vmem,
-        scratch_shapes=[pltpu.VMEM((chips, pair, 2, lines, states), jnp.float32)],
+        scratch_shapes=[pltpu.VMEM((blocks.shape[1], blocks.shape[0], lines, depth), jnp.float32)],
         compiler_params=pltpu.CompilerParams(vmem_limit_bytes=16 << 20),
         cost_estimate=pl.CostEstimate(
-            flops=2 * (rows + depth) * depth * states * energies,
-            bytes_accessed=4 * (3 * freq.size + energies * states * states),
+            flops=omega.size * depth * energies,
+            bytes_accessed=4 * (2 * omega.size + blocks.size + energies * depth * depth),
             transcendentals=0,
         ),
-    )(place, shifts, omega, freq, mine, other, right_cols)
+    )(place, shifts, omega, freq, blocks, *more)
 
 
 def exchange(pieces, axes, first):
@@ -90,17 +99,22 @@
     energies = eval_energy.shape[0]
     states = mtx_left.shape[2]
     depth = pole_freq.shape[1]
+    place = jnp.stack([lax.axis_index("z_lo"), lax.axis_index("core")])
+    pairs = (-1, 2, mtx_left.shape[1], depth)
+    omega, freq = omega_sq.reshape(pairs), pole_freq.reshape(pairs)
     hits = (band_ids[:, None] == jnp.arange(table, dtype=jnp.int32)[None, :]).astype(jnp.float32)
     levels = jnp.sum(hits * band_energy[None, :], axis=1)
     shifts = eval_energy[None, :] - levels[:, None]
     shift_rows = jnp.broadcast_to(shifts[0][:, None, None], (energies, 8, depth))
-    place = jnp.stack([lax.axis_index("z_lo"), lax.axis_index("core")])
     left_far = gather(mtx_left[0], "z_far", FAR_FIRST)
     mine = with_partner(left_far, "z_lo")
     other = lax.ppermute(mine, "core", ((0, 1), (1, 0)))
     right_blocks = gather(mtx_right[0], ROW, ROW_FIRST)
     right_cols = jnp.roll(right_blocks, ROW_FIRST, axis=0).reshape(-1, states)
-    total = block_sum(place, shift_rows, omega_sq, pole_freq, mine, other, right_cols)
+    arrays = (place, shift_rows, omega, freq)
+    part = local_kernel(mine_body, (energies, states, depth), *arrays, mine)
+    shape = (states, energies * states)
+    total = local_kernel(rest_body, shape, *arrays, other, part, right_cols)
     return sum_everywhere(total)
 
 

time: 119 us -> 118 us (level)
    pallas_call x1 -> x2, Pallas kernels: 2 us -> 2.75 us  [local_kernel(): pl.pallas_call(body, out_shape=jax.ShapeDtypeStruct(out_shape, jnp.float3...]
  transfers between devices with their start and end apart: 4 -> 4, of which waited for: 3 -> 2; matrix products, arithmetic and copies ran while one was open for 1% -> 1% of each run, Pallas kernels for 0% -> 1%
where the time goes in v6:
time: 118 us
  starting transfers between devices  51.1 us (43%)
  blocking collectives  51.1 us (43%)
  waiting for transfers between devices  7.72 us (7%)
  local copies, waits for them, and re-layouts  3.04 us (3%)
  Pallas kernels  2.75 us (2%)
  other arithmetic  1.46 us (1%)
    all_to_all x3, blocking collectives, exchange(): return lax.all_to_all(pieces, axes, 0, 0, axis_index_groups=[order])  51.1 us
    all_to_all x2, starting transfers between devices, exchange(): return lax.all_to_all(pieces, axes, 0, 0, axis_index_groups=[order])  44.5 us
    all_to_all x2, waiting for transfers between devices, exchange(): return lax.all_to_all(pieces, axes, 0, 0, axis_index_groups=[order])  5.36 us
    ppermute x1, starting transfers between devices, shards(): other = lax.ppermute(mine, 'core', ((0, 1), (1, 0)))  4.55 us
    pallas_call x2, Pallas kernels, local_kernel(): pl.pallas_call(body, out_shape=jax.ShapeDtypeStruct(out_shape, jnp.float3...  2.75 us
  transfers between devices with their start and end apart: 4, of which 2 were waited for; matrix products, arithmetic and copies ran while one was open for 1% of the time, Pallas kernels for 1%

profile of v6, /device:TPU:1, one launch (start us, length us, event | category | flops | bytes accessed | tf_op | source)
XLA Modules:
  0.0 117.9 jit_solution(18369754450627778955)
XLA Ops:
  0.0 1.3 %broadcast_in_dim.11 = f32[16,8,128]{2,1,0:T(8,128)} broadcast(f32[8,128]{1,0:T(8,128)} %bitcast.18), dimensions={1,2} | broadcast | bytes 69632 | tf_op jit(solution)/shard_map/broadcast_in_dim | solution.py:82
  1.3 0.0 copy-start.3
  1.3 35.7 %all-to-all-start = ((f32[16,8,128]{2,1,0:T(8,128)}), f32[16,8,128]{2,1,0:T(8,128)S(1)}, u32[]{:S(2)}, u32[]{:S(2)}) async-start(f32[16,8,128]{2,1,0:T(8,128)} %broadcast_in_dim.11), calls=%async_computation | async-start | bytes 131072 | tf_op jit(solution)/shard_map/all_to_all | solution.py:77
  37.0 0.0 copy-start.2
  37.7 0.0 copy-done.3
  37.7 0.6 fusion
  38.3 5.4 %all-to-all-done = f32[16,8,128]{2,1,0:T(8,128)S(1)} async-done(((f32[16,8,128]{2,1,0:T(8,128)}), f32[16,8,128]{2,1,0:T(8,128)S(1)}, u32[]{:S(2)}, u32[]{:S(2)}) %all-to-all-start) | async-done | bytes 65568 | tf_op jit(solution)/shard_map/all_to_all | solution.py:77
  43.7 0.0 copy-done.2
  43.7 0.6 broadcast_in_dim.24
  44.3 0.0 copy-start.4
  44.3 8.8 %all-to-all-start.1 = ((f32[16,8,128]{2,1,0:T(8,128)}), f32[16,8,128]{2,1,0:T(8,128)S(1)}, u32[]{:S(2)}, u32[]{:S(2)}) async-start(f32[16,8,128]{2,1,0:T(8,128)} %broadcast_in_dim.24), calls=%async_computation.1 | async-start | bytes 131072 | tf_op jit(solution)/shard_map/all_to_all | solution.py:77
  53.1 2.0 %collective-permute-start = (f32[16,8,128]{2,1,0:T(8,128)S(1)}, f32[16,8,128]{2,1,0:T(8,128)S(1)}, u32[]{:S(2)}, u32[]{:S(2)}) collective-permute-start(f32[16,8,128]{2,1,0:T(8,128)S(1)} %all-to-all-done), channel_id=1, source_target_pairs={{0,2},{2,0},{1,3},{3,1},{4,6},{6,4},{5,7},{7,5},{8,10},{10,8},{9,1... | collective-permute-start | bytes 196616 | tf_op jit(solution)/shard_map/ppermute | solution.py:94
  55.1 0.0 copy-done.4
  55.2 0.6 broadcast_subtract_fusion
  55.8 2.4 %collective-permute-done = f32[16,8,128]{2,1,0:T(8,128)S(1)} collective-permute-done((f32[16,8,128]{2,1,0:T(8,128)S(1)}, f32[16,8,128]{2,1,0:T(8,128)S(1)}, u32[]{:S(2)}, u32[]{:S(2)}) %collective-permute-start) | collective-permute-done | bytes 65568 | tf_op jit(solution)/shard_map/ppermute | solution.py:94
  58.1 0.0 copy-start
  58.1 0.0 copy-start.1
  58.1 4.5 %collective-permute-start.1 = (f32[2,16,8,128]{3,2,1,0:T(8,128)S(1)}, f32[2,16,8,128]{3,2,1,0:T(8,128)S(1)}, u32[]{:S(2)}, u32[]{:S(2)}) collective-permute-start(f32[2,16,8,128]{3,2,1,0:T(8,128)S(1)} %pad_maximum_fusion.mine_ref), channel_id=1, source_target_pairs={{0,1},{1,0},{2,3},{3,2},{4,5},{5,4},{6,7},{7,6},{8,9},{9,8},{10,11... | collective-permute-start | bytes 393224 | tf_op jit(solution)/shard_map/ppermute | solution.py:111
  62.7 0.1 pad_add_fusion.place_ref
  62.8 0.0 all-to-all-done.1
  62.8 0.1 broadcast_in_dim.10.shift_ref
  62.9 0.0 copy-done
  62.9 0.0 copy-done.1
  62.9 1.1 shard_map.73.part_ref
  64.0 0.0 collective-permute-done.1.other_ref
  64.0 1.7 %shard_map.74 = f32[128,384]{1,0:T(8,128)S(1)} custom-call(s32[2]{0:T(128)S(1)} %pad_add_fusion.place_ref, f32[3,8,128]{2,1,0:T(8,128)S(1)} %broadcast_in_dim.10.shift_ref, f32[32,2,8,128]{3,2,1,0:T(8,128)S(1)} %bitcast.13, f32[32,2,8,128]{3,2,1,0:T(8,128)S(1)} %bitcast.15, f32[2,16,8,128]{3,2,1,0:T(8,128)S(1)} %collective-permute-done.1.other_ref, ...), custom_call_target="tpu_custom_call" | custom-call | flops 25165824 | bytes 851968 | tf_op jit(solution)/shard_map/pallas_call | solution.py:59
  65.7 0.1 reshape.32
  65.8 11.8 %all_to_all.25 = f32[64,2,384]{2,1,0:T(2,128)S(1)} all-to-all(f32[64,2,384]{2,1,0:T(2,128)S(1)} %reshape.32), channel_id=1, replica_groups={{642,643,704,705,706,707,768,769,770,771,832,833,834,835,896,897,898,89..., dimensions={0} | all-to-all | bytes 393216 | tf_op jit(solution)/shard_map/all_to_all | solution.py:77
  77.5 0.1 reduce_sum.28
  77.7 26.5 %all_to_all.26 = f32[16,2,384]{2,1,0:T(2,128)S(1)} all-to-all(f32[16,2,384]{2,1,0:T(2,128)S(1)} %broadcast_in_dim.25), channel_id=1, replica_groups={{32,36,40,44,48,52,56,60,0,4,8,12,16,20,24,28},{33,37,41,45,49,53,57,61..., dimensions={0} | all-to-all | bytes 98304 | tf_op jit(solution)/shard_map/all_to_all | solution.py:77
  104.2 0.1 broadcast_in_dim.26
  104.2 12.9 %all_to_all.27 = f32[64,2,384]{2,1,0:T(2,128)S(1)} all-to-all(f32[64,2,384]{2,1,0:T(2,128)S(1)} %broadcast_in_dim.26), channel_id=1, replica_groups={{642,643,704,705,706,707,768,769,770,771,832,833,834,835,896,897,898,89..., dimensions={0} | all-to-all | bytes 393216 | tf_op jit(solution)/shard_map/all_to_all | solution.py:77
  117.1 0.8 reshape.33
  (6 shorter events, 0.1 us)
Async XLA Ops:
  1.3 36.3 %copy-start.3 = (f32[64]{0:T(128)S(1)}, f32[64]{0:T(128)}, u32[]{:S(2)}) copy-start(f32[64]{0:T(128)} %param.12) | copy-start | bytes 772
  1.3 42.3 %all-to-all-start = ((f32[16,8,128]{2,1,0:T(8,128)}), f32[16,8,128]{2,1,0:T(8,128)S(1)}, u32[]{:S(2)}, u32[]{:S(2)}) async-start(f32[16,8,128]{2,1,0:T(8,128)} %broadcast_in_dim.11), calls=%async_computation | async-start | bytes 131072 | tf_op jit(solution)/shard_map/all_to_all | solution.py:77
  37.0 6.7 %copy-start.2 = (f32[1,8,128]{2,1,0:T(8,128)S(1)}, f32[1,8,128]{2,1,0:T(8,128)}, u32[]{:S(2)}) copy-start(f32[1,8,128]{2,1,0:T(8,128)} %param.10) | copy-start | bytes 12292
  44.3 10.8 %copy-start.4 = (f32[3]{0:T(128)S(1)}, f32[3]{0:T(128)}, u32[]{:S(2)}) copy-start(f32[3]{0:T(128)} %param.13) | copy-start | bytes 40
  44.3 18.5 %all-to-all-start.1 = ((f32[16,8,128]{2,1,0:T(8,128)}), f32[16,8,128]{2,1,0:T(8,128)S(1)}, u32[]{:S(2)}, u32[]{:S(2)}) async-start(f32[16,8,128]{2,1,0:T(8,128)} %broadcast_in_dim.24), calls=%async_computation.1 | async-start | bytes 131072 | tf_op jit(solution)/shard_map/all_to_all | solution.py:77
  53.1 5.0 %collective-permute-start = (f32[16,8,128]{2,1,0:T(8,128)S(1)}, f32[16,8,128]{2,1,0:T(8,128)S(1)}, u32[]{:S(2)}, u32[]{:S(2)}) collective-permute-start(f32[16,8,128]{2,1,0:T(8,128)S(1)} %all-to-all-done), channel_id=1, source_target_pairs={{0,2},{2,0},{1,3},{3,1},{4,6},{6,4},{5,7},{7,5},{8,10},{10,8},{9,1... | collective-permute-start | bytes 196616 | tf_op jit(solution)/shard_map/ppermute | solution.py:94
  58.1 4.8 %copy-start = (f32[512,128]{1,0:T(8,128)S(1)}, f32[512,128]{1,0:T(8,128)}, u32[]{:S(2)}) copy-start(f32[512,128]{1,0:T(8,128)} %param.7) | copy-start | bytes 786436
  58.1 4.8 %copy-start.1 = (f32[512,128]{1,0:T(8,128)S(1)}, f32[512,128]{1,0:T(8,128)}, u32[]{:S(2)}) copy-start(f32[512,128]{1,0:T(8,128)} %param.8) | copy-start | bytes 786436
  58.1 5.8 %collective-permute-start.1 = (f32[2,16,8,128]{3,2,1,0:T(8,128)S(1)}, f32[2,16,8,128]{3,2,1,0:T(8,128)S(1)}, u32[]{:S(2)}, u32[]{:S(2)}) collective-permute-start(f32[2,16,8,128]{3,2,1,0:T(8,128)S(1)} %pad_maximum_fusion.mine_ref), channel_id=1, source_target_pairs={{0,1},{1,0},{2,3},{3,2},{4,5},{5,4},{6,7},{7,6},{8,9},{9,8},{10,11... | collective-permute-start | bytes 393224 | tf_op jit(solution)/shard_map/ppermute | solution.py:111

commit v7 on v6

--- a/solution.py
+++ b/solution.py
@@ -44,12 +44,35 @@
         out_ref[energy] = term
 
 
-def rest_body(place_ref, shift_ref, omega_ref, freq_ref, other_ref, part_ref, right_ref, out_ref, left_ref):
+def rest_body(place_ref, shift_ref, omega_ref, freq_ref, other_ref, part_ref, out_ref, left_ref):
     z_lo, core = place_ref[0], place_ref[1]
-    states = right_ref.shape[1]
     terms = half_terms(z_lo, 1 - core, shift_ref, omega_ref, freq_ref, other_ref, left_ref)
     for energy, term in enumerate(terms):
-        out_ref[:, energy * states : (energy + 1) * states] = dot(part_ref[energy] + term, right_ref[...])
+        out_ref[energy] = part_ref[energy] + term
+
+
+def last_body(part_ref, right_ref, out_ref):
+    states = right_ref.shape[1]
+    for energy in range(part_ref.shape[0]):
+        out_ref[:, energy * states : (energy + 1) * states] = dot(part_ref[energy], right_ref[...])
+
+
+def last_kernel(part, right_cols):
+    energies, states, _ = part.shape
+    vmem = pl.BlockSpec(memory_space=pltpu.VMEM)
+    return pl.pallas_call(
+        last_body,
+        name="last",
+        out_shape=jax.ShapeDtypeStruct((states, energies * right_cols.shape[1]), jnp.float32),
+        in_specs=[vmem, vmem],
+        out_specs=vmem,
+        compiler_params=pltpu.CompilerParams(vmem_limit_bytes=16 << 20),
+        cost_estimate=pl.CostEstimate(
+            flops=2 * part.size * right_cols.shape[1],
+            bytes_accessed=4 * (2 * part.size + right_cols.size),
+            transcendentals=0,
+        ),
+    )(part, right_cols)
 
 
 def local_kernel(body, out_shape, place, shifts, omega, freq, blocks, *more):
@@ -113,8 +136,8 @@
     right_cols = jnp.roll(right_blocks, ROW_FIRST, axis=0).reshape(-1, states)
     arrays = (place, shift_rows, omega, freq)
     part = local_kernel(mine_body, (energies, states, depth), *arrays, mine)
-    shape = (states, energies * states)
-    total = local_kernel(rest_body, shape, *arrays, other, part, right_cols)
+    part = local_kernel(rest_body, part.shape, *arrays, other, part)
+    total = last_kernel(part, right_cols)
     return sum_everywhere(total)
 
 

time: 118 us -> 118 us (level)
  no operation moved by 1% of the time
where the time goes in v7:
time: 118 us
  starting transfers between devices  51.1 us (43%)
  blocking collectives  51.1 us (43%)
  waiting for transfers between devices  7.72 us (7%)
  local copies, waits for them, and re-layouts  3.04 us (3%)
  Pallas kernels  2.48 us (2%)
  other arithmetic  1.46 us (1%)
    all_to_all x3, blocking collectives, exchange(): return lax.all_to_all(pieces, axes, 0, 0, axis_index_groups=[order])  51.1 us
    all_to_all x2, starting transfers between devices, exchange(): return lax.all_to_all(pieces, axes, 0, 0, axis_index_groups=[order])  44.5 us
    all_to_all x2, waiting for transfers between devices, exchange(): return lax.all_to_all(pieces, axes, 0, 0, axis_index_groups=[order])  5.36 us
    ppermute x1, starting transfers between devices, shards(): other = lax.ppermute(mine, 'core', ((0, 1), (1, 0)))  4.55 us
  transfers between devices with their start and end apart: 4, of which 2 were waited for; matrix products, arithmetic and copies ran while one was open for 1% of the time, Pallas kernels for 1%

profile of v7, /device:TPU:1, one launch (start us, length us, event | category | flops | bytes accessed | tf_op | source)
XLA Modules:
  0.0 117.6 jit_solution(4448237861301263191)
XLA Ops:
  0.0 1.3 %broadcast_in_dim.11 = f32[16,8,128]{2,1,0:T(8,128)} broadcast(f32[8,128]{1,0:T(8,128)} %bitcast.18), dimensions={1,2} | broadcast | bytes 69632 | tf_op jit(solution)/shard_map/broadcast_in_dim | solution.py:105
  1.3 0.0 copy-start.3
  1.3 35.7 %all-to-all-start = ((f32[16,8,128]{2,1,0:T(8,128)}), f32[16,8,128]{2,1,0:T(8,128)S(1)}, u32[]{:S(2)}, u32[]{:S(2)}) async-start(f32[16,8,128]{2,1,0:T(8,128)} %broadcast_in_dim.11), calls=%async_computation | async-start | bytes 131072 | tf_op jit(solution)/shard_map/all_to_all | solution.py:100
  37.0 0.0 copy-start.2
  37.7 0.0 copy-done.3
  37.7 0.6 fusion
  38.3 5.4 %all-to-all-done = f32[16,8,128]{2,1,0:T(8,128)S(1)} async-done(((f32[16,8,128]{2,1,0:T(8,128)}), f32[16,8,128]{2,1,0:T(8,128)S(1)}, u32[]{:S(2)}, u32[]{:S(2)}) %all-to-all-start) | async-done | bytes 65568 | tf_op jit(solution)/shard_map/all_to_all | solution.py:100
  43.7 0.0 copy-done.2
  43.7 0.6 broadcast_in_dim.24
  44.3 0.0 copy-start.4
  44.3 8.8 %all-to-all-start.1 = ((f32[16,8,128]{2,1,0:T(8,128)}), f32[16,8,128]{2,1,0:T(8,128)S(1)}, u32[]{:S(2)}, u32[]{:S(2)}) async-start(f32[16,8,128]{2,1,0:T(8,128)} %broadcast_in_dim.24), calls=%async_computation.1 | async-start | bytes 131072 | tf_op jit(solution)/shard_map/all_to_all | solution.py:100
  53.1 2.0 %collective-permute-start = (f32[16,8,128]{2,1,0:T(8,128)S(1)}, f32[16,8,128]{2,1,0:T(8,128)S(1)}, u32[]{:S(2)}, u32[]{:S(2)}) collective-permute-start(f32[16,8,128]{2,1,0:T(8,128)S(1)} %all-to-all-done), channel_id=1, source_target_pairs={{0,2},{2,0},{1,3},{3,1},{4,6},{6,4},{5,7},{7,5},{8,10},{10,8},{9,1... | collective-permute-start | bytes 196616 | tf_op jit(solution)/shard_map/ppermute | solution.py:117
  55.1 0.0 copy-done.4
  55.2 0.6 broadcast_subtract_fusion
  55.8 2.4 %collective-permute-done = f32[16,8,128]{2,1,0:T(8,128)S(1)} collective-permute-done((f32[16,8,128]{2,1,0:T(8,128)S(1)}, f32[16,8,128]{2,1,0:T(8,128)S(1)}, u32[]{:S(2)}, u32[]{:S(2)}) %collective-permute-start) | collective-permute-done | bytes 65568 | tf_op jit(solution)/shard_map/ppermute | solution.py:117
  58.1 0.0 copy-start
  58.1 0.0 copy-start.1
  58.1 4.5 %collective-permute-start.1 = (f32[2,16,8,128]{3,2,1,0:T(8,128)S(1)}, f32[2,16,8,128]{3,2,1,0:T(8,128)S(1)}, u32[]{:S(2)}, u32[]{:S(2)}) collective-permute-start(f32[2,16,8,128]{3,2,1,0:T(8,128)S(1)} %pad_maximum_fusion.mine_ref), channel_id=1, source_target_pairs={{0,1},{1,0},{2,3},{3,2},{4,5},{5,4},{6,7},{7,6},{8,9},{9,8},{10,11... | collective-permute-start | bytes 393224 | tf_op jit(solution)/shard_map/ppermute | solution.py:134
  62.7 0.1 pad_add_fusion.place_ref
  62.8 0.0 all-to-all-done.1
  62.8 0.1 broadcast_in_dim.10.shift_ref
  62.9 0.0 copy-done
  62.9 0.0 copy-done.1
  62.9 1.1 shard_map.73.part_ref
  64.0 0.0 collective-permute-done.1.other_ref
  64.0 1.1 shard_map.74.part_ref
  65.1 0.3 last.1
  65.4 0.1 reshape.32
  65.5 11.8 %all_to_all.25 = f32[64,2,384]{2,1,0:T(2,128)S(1)} all-to-all(f32[64,2,384]{2,1,0:T(2,128)S(1)} %reshape.32), channel_id=1, replica_groups={{642,643,704,705,706,707,768,769,770,771,832,833,834,835,896,897,898,89..., dimensions={0} | all-to-all | bytes 393216 | tf_op jit(solution)/shard_map/all_to_all | solution.py:100
  77.3 0.1 reduce_sum.28
  77.4 26.5 %all_to_all.26 = f32[16,2,384]{2,1,0:T(2,128)S(1)} all-to-all(f32[16,2,384]{2,1,0:T(2,128)S(1)} %broadcast_in_dim.25), channel_id=1, replica_groups={{32,36,40,44,48,52,56,60,0,4,8,12,16,20,24,28},{33,37,41,45,49,53,57,61..., dimensions={0} | all-to-all | bytes 98304 | tf_op jit(solution)/shard_map/all_to_all | solution.py:100
  103.9 0.1 broadcast_in_dim.26
  104.0 12.9 %all_to_all.27 = f32[64,2,384]{2,1,0:T(2,128)S(1)} all-to-all(f32[64,2,384]{2,1,0:T(2,128)S(1)} %broadcast_in_dim.26), channel_id=1, replica_groups={{642,643,704,705,706,707,768,769,770,771,832,833,834,835,896,897,898,89..., dimensions={0} | all-to-all | bytes 393216 | tf_op jit(solution)/shard_map/all_to_all | solution.py:100
  116.8 0.8 reshape.33
  (6 shorter events, 0.1 us)
Async XLA Ops:
  1.3 36.3 %copy-start.3 = (f32[64]{0:T(128)S(1)}, f32[64]{0:T(128)}, u32[]{:S(2)}) copy-start(f32[64]{0:T(128)} %param.12) | copy-start | bytes 772
  1.3 42.3 %all-to-all-start = ((f32[16,8,128]{2,1,0:T(8,128)}), f32[16,8,128]{2,1,0:T(8,128)S(1)}, u32[]{:S(2)}, u32[]{:S(2)}) async-start(f32[16,8,128]{2,1,0:T(8,128)} %broadcast_in_dim.11), calls=%async_computation | async-start | bytes 131072 | tf_op jit(solution)/shard_map/all_to_all | solution.py:100
  37.0 6.7 %copy-start.2 = (f32[1,8,128]{2,1,0:T(8,128)S(1)}, f32[1,8,128]{2,1,0:T(8,128)}, u32[]{:S(2)}) copy-start(f32[1,8,128]{2,1,0:T(8,128)} %param.10) | copy-start | bytes 12292
  44.3 10.8 %copy-start.4 = (f32[3]{0:T(128)S(1)}, f32[3]{0:T(128)}, u32[]{:S(2)}) copy-start(f32[3]{0:T(128)} %param.13) | copy-start | bytes 40
  44.3 18.5 %all-to-all-start.1 = ((f32[16,8,128]{2,1,0:T(8,128)}), f32[16,8,128]{2,1,0:T(8,128)S(1)}, u32[]{:S(2)}, u32[]{:S(2)}) async-start(f32[16,8,128]{2,1,0:T(8,128)} %broadcast_in_dim.24), calls=%async_computation.1 | async-start | bytes 131072 | tf_op jit(solution)/shard_map/all_to_all | solution.py:100
  53.1 5.0 %collective-permute-start = (f32[16,8,128]{2,1,0:T(8,128)S(1)}, f32[16,8,128]{2,1,0:T(8,128)S(1)}, u32[]{:S(2)}, u32[]{:S(2)}) collective-permute-start(f32[16,8,128]{2,1,0:T(8,128)S(1)} %all-to-all-done), channel_id=1, source_target_pairs={{0,2},{2,0},{1,3},{3,1},{4,6},{6,4},{5,7},{7,5},{8,10},{10,8},{9,1... | collective-permute-start | bytes 196616 | tf_op jit(solution)/shard_map/ppermute | solution.py:117
  58.1 4.8 %copy-start = (f32[512,128]{1,0:T(8,128)S(1)}, f32[512,128]{1,0:T(8,128)}, u32[]{:S(2)}) copy-start(f32[512,128]{1,0:T(8,128)} %param.7) | copy-start | bytes 786436
  58.1 4.8 %copy-start.1 = (f32[512,128]{1,0:T(8,128)S(1)}, f32[512,128]{1,0:T(8,128)}, u32[]{:S(2)}) copy-start(f32[512,128]{1,0:T(8,128)} %param.8) | copy-start | bytes 786436
  58.1 5.8 %collective-permute-start.1 = (f32[2,16,8,128]{3,2,1,0:T(8,128)S(1)}, f32[2,16,8,128]{3,2,1,0:T(8,128)S(1)}, u32[]{:S(2)}, u32[]{:S(2)}) collective-permute-start(f32[2,16,8,128]{3,2,1,0:T(8,128)S(1)} %pad_maximum_fusion.mine_ref), channel_id=1, source_target_pairs={{0,1},{1,0},{2,3},{3,2},{4,5},{5,4},{6,7},{7,6},{8,9},{9,8},{10,11... | collective-permute-start | bytes 393224 | tf_op jit(solution)/shard_map/ppermute | solution.py:134

commit v8 on v7

--- a/solution.py
+++ b/solution.py
@@ -52,9 +52,9 @@
 
 
 def last_body(part_ref, right_ref, out_ref):
-    states = right_ref.shape[1]
+    lines, lanes = out_ref.shape[2:]
     for energy in range(part_ref.shape[0]):
-        out_ref[:, energy * states : (energy + 1) * states] = dot(part_ref[energy], right_ref[...])
+        out_ref[:, energy] = dot(part_ref[energy], right_ref[...]).reshape(-1, lines, lanes)
 
 
 def last_kernel(part, right_cols):
@@ -63,7 +63,7 @@
     return pl.pallas_call(
         last_body,
         name="last",
-        out_shape=jax.ShapeDtypeStruct((states, energies * right_cols.shape[1]), jnp.float32),
+        out_shape=jax.ShapeDtypeStruct((states // 8, energies, 8, right_cols.shape[1]), jnp.float32),
         in_specs=[vmem, vmem],
         out_specs=vmem,
         compiler_params=pltpu.CompilerParams(vmem_limit_bytes=16 << 20),
@@ -105,12 +105,12 @@
     return exchange(jnp.broadcast_to(block, (size, *block.shape)), axes, first)
 
 
-def sum_everywhere(total):
-    rows, columns = total.shape
+def sum_everywhere(tiles):
     size = lax.axis_size(NEAR)
-    pieces = exchange(total.reshape(size, rows // size, columns), NEAR, NEAR_FIRST)
+    lanes = tiles.shape[-1]
+    pieces = exchange(tiles.reshape(size, -1, 2, lanes), NEAR, NEAR_FIRST)
     piece = jnp.sum(gather(jnp.sum(pieces, axis=0), "z_far", FAR_FIRST), axis=0)
-    return gather(piece, NEAR, NEAR_FIRST).reshape(rows, columns)
+    return gather(piece, NEAR, NEAR_FIRST).reshape(tiles.shape)
 
 
 def with_partner(blocks, axis):
@@ -137,8 +137,8 @@
     arrays = (place, shift_rows, omega, freq)
     part = local_kernel(mine_body, (energies, states, depth), *arrays, mine)
     part = local_kernel(rest_body, part.shape, *arrays, other, part)
-    total = last_kernel(part, right_cols)
-    return sum_everywhere(total)
+    tiles = last_kernel(part, right_cols)
+    return sum_everywhere(tiles).transpose(0, 2, 1, 3).reshape(states, energies * states)
 
 
 def solution(mesh):

time: 118 us -> 118 us (level)
  no operation moved by 1% of the time
where the time goes in v8:
time: 118 us; the launch traced here: 117 us
  starting transfers between devices  51.1 us (43%)
  blocking collectives  51.1 us (43%)
  waiting for transfers between devices  7.72 us (7%)
  local copies, waits for them, and re-layouts  2.8 us (2%)
  Pallas kernels  2.48 us (2%)
  other arithmetic  1.46 us (1%)
    all_to_all x3, blocking collectives, exchange(): return lax.all_to_all(pieces, axes, 0, 0, axis_index_groups=[order])  51.1 us
    all_to_all x2, starting transfers between devices, exchange(): return lax.all_to_all(pieces, axes, 0, 0, axis_index_groups=[order])  44.5 us
    all_to_all x2, waiting for transfers between devices, exchange(): return lax.all_to_all(pieces, axes, 0, 0, axis_index_groups=[order])  5.36 us
    ppermute x1, starting transfers between devices, shards(): other = lax.ppermute(mine, 'core', ((0, 1), (1, 0)))  4.55 us
  transfers between devices with their start and end apart: 4, of which 2 were waited for; matrix products, arithmetic and copies ran while one was open for 1% of the time, Pallas kernels for 1%

profile of v8, /device:TPU:1, one launch (start us, length us, event | category | flops | bytes accessed | tf_op | source)
XLA Modules:
  0.0 117.4 jit_solution(5430787430914580517)
XLA Ops:
  0.0 1.3 %broadcast_in_dim.11 = f32[16,8,128]{2,1,0:T(8,128)} broadcast(f32[8,128]{1,0:T(8,128)} %bitcast.26), dimensions={1,2} | broadcast | bytes 69632 | tf_op jit(solution)/shard_map/broadcast_in_dim | solution.py:105
  1.3 0.0 copy-start.3
  1.3 35.7 %all-to-all-start = ((f32[16,8,128]{2,1,0:T(8,128)}), f32[16,8,128]{2,1,0:T(8,128)S(1)}, u32[]{:S(2)}, u32[]{:S(2)}) async-start(f32[16,8,128]{2,1,0:T(8,128)} %broadcast_in_dim.11), calls=%async_computation | async-start | bytes 131072 | tf_op jit(solution)/shard_map/all_to_all | solution.py:100
  37.0 0.0 copy-start.2
  37.7 0.0 copy-done.3
  37.7 0.6 fusion
  38.3 5.4 %all-to-all-done = f32[16,8,128]{2,1,0:T(8,128)S(1)} async-done(((f32[16,8,128]{2,1,0:T(8,128)}), f32[16,8,128]{2,1,0:T(8,128)S(1)}, u32[]{:S(2)}, u32[]{:S(2)}) %all-to-all-start) | async-done | bytes 65568 | tf_op jit(solution)/shard_map/all_to_all | solution.py:100
  43.7 0.0 copy-done.2
  43.7 0.6 broadcast_in_dim.24
  44.3 0.0 copy-start.4
  44.3 8.8 %all-to-all-start.1 = ((f32[16,8,128]{2,1,0:T(8,128)}), f32[16,8,128]{2,1,0:T(8,128)S(1)}, u32[]{:S(2)}, u32[]{:S(2)}) async-start(f32[16,8,128]{2,1,0:T(8,128)} %broadcast_in_dim.24), calls=%async_computation.1 | async-start | bytes 131072 | tf_op jit(solution)/shard_map/all_to_all | solution.py:100
  53.1 2.0 %collective-permute-start = (f32[16,8,128]{2,1,0:T(8,128)S(1)}, f32[16,8,128]{2,1,0:T(8,128)S(1)}, u32[]{:S(2)}, u32[]{:S(2)}) collective-permute-start(f32[16,8,128]{2,1,0:T(8,128)S(1)} %all-to-all-done), channel_id=1, source_target_pairs={{0,2},{2,0},{1,3},{3,1},{4,6},{6,4},{5,7},{7,5},{8,10},{10,8},{9,1... | collective-permute-start | bytes 196616 | tf_op jit(solution)/shard_map/ppermute | solution.py:117
  55.1 0.0 copy-done.4
  55.2 0.6 broadcast_subtract_fusion
  55.8 2.4 %collective-permute-done = f32[16,8,128]{2,1,0:T(8,128)S(1)} collective-permute-done((f32[16,8,128]{2,1,0:T(8,128)S(1)}, f32[16,8,128]{2,1,0:T(8,128)S(1)}, u32[]{:S(2)}, u32[]{:S(2)}) %collective-permute-start) | collective-permute-done | bytes 65568 | tf_op jit(solution)/shard_map/ppermute | solution.py:117
  58.1 0.0 copy-start
  58.1 0.0 copy-start.1
  58.1 4.5 %collective-permute-start.1 = (f32[2,16,8,128]{3,2,1,0:T(8,128)S(1)}, f32[2,16,8,128]{3,2,1,0:T(8,128)S(1)}, u32[]{:S(2)}, u32[]{:S(2)}) collective-permute-start(f32[2,16,8,128]{3,2,1,0:T(8,128)S(1)} %pad_maximum_fusion.mine_ref), channel_id=1, source_target_pairs={{0,1},{1,0},{2,3},{3,2},{4,5},{5,4},{6,7},{7,6},{8,9},{9,8},{10,11... | collective-permute-start | bytes 393224 | tf_op jit(solution)/shard_map/ppermute | solution.py:134
  62.7 0.1 pad_add_fusion.place_ref
  62.8 0.0 all-to-all-done.1
  62.8 0.1 broadcast_in_dim.10.shift_ref
  62.9 0.0 copy-done
  62.9 0.0 copy-done.1
  62.9 1.1 shard_map.73.part_ref
  64.0 0.0 collective-permute-done.1.other_ref
  64.0 1.1 shard_map.74.part_ref
  65.1 0.3 last.1
  65.4 11.8 %all_to_all.25 = f32[64,3,2,128]{3,2,1,0:T(2,128)S(1)} all-to-all(f32[64,3,2,128]{3,2,1,0:T(2,128)S(1)} %bitcast.22), channel_id=1, replica_groups={{642,643,704,705,706,707,768,769,770,771,832,833,834,835,896,897,898,89..., dimensions={0} | all-to-all | bytes 393216 | tf_op jit(solution)/shard_map/all_to_all | solution.py:100
  77.2 0.1 reduce_sum.28
  77.3 26.5 %all_to_all.26 = f32[16,3,2,128]{3,2,1,0:T(2,128)S(1)} all-to-all(f32[16,3,2,128]{3,2,1,0:T(2,128)S(1)} %broadcast_in_dim.25), channel_id=1, replica_groups={{32,36,40,44,48,52,56,60,0,4,8,12,16,20,24,28},{33,37,41,45,49,53,57,61..., dimensions={0} | all-to-all | bytes 98304 | tf_op jit(solution)/shard_map/all_to_all | solution.py:100
  103.8 0.1 broadcast_in_dim.26
  103.8 12.9 %all_to_all.27 = f32[64,3,2,128]{3,2,1,0:T(2,128)S(1)} all-to-all(f32[64,3,2,128]{3,2,1,0:T(2,128)S(1)} %broadcast_in_dim.26), channel_id=1, replica_groups={{642,643,704,705,706,707,768,769,770,771,832,833,834,835,896,897,898,89..., dimensions={0} | all-to-all | bytes 393216 | tf_op jit(solution)/shard_map/all_to_all | solution.py:100
  116.7 0.7 copy.12
  (6 shorter events, 0.1 us)
Async XLA Ops:
  1.3 36.3 %copy-start.3 = (f32[64]{0:T(128)S(1)}, f32[64]{0:T(128)}, u32[]{:S(2)}) copy-start(f32[64]{0:T(128)} %param.12) | copy-start | bytes 772
  1.3 42.3 %all-to-all-start = ((f32[16,8,128]{2,1,0:T(8,128)}), f32[16,8,128]{2,1,0:T(8,128)S(1)}, u32[]{:S(2)}, u32[]{:S(2)}) async-start(f32[16,8,128]{2,1,0:T(8,128)} %broadcast_in_dim.11), calls=%async_computation | async-start | bytes 131072 | tf_op jit(solution)/shard_map/all_to_all | solution.py:100
  37.0 6.7 %copy-start.2 = (f32[1,8,128]{2,1,0:T(8,128)S(1)}, f32[1,8,128]{2,1,0:T(8,128)}, u32[]{:S(2)}) copy-start(f32[1,8,128]{2,1,0:T(8,128)} %param.10) | copy-start | bytes 12292
  44.3 10.8 %copy-start.4 = (f32[3]{0:T(128)S(1)}, f32[3]{0:T(128)}, u32[]{:S(2)}) copy-start(f32[3]{0:T(128)} %param.13) | copy-start | bytes 40
  44.3 18.5 %all-to-all-start.1 = ((f32[16,8,128]{2,1,0:T(8,128)}), f32[16,8,128]{2,1,0:T(8,128)S(1)}, u32[]{:S(2)}, u32[]{:S(2)}) async-start(f32[16,8,128]{2,1,0:T(8,128)} %broadcast_in_dim.24), calls=%async_computation.1 | async-start | bytes 131072 | tf_op jit(solution)/shard_map/all_to_all | solution.py:100
  53.1 5.0 %collective-permute-start = (f32[16,8,128]{2,1,0:T(8,128)S(1)}, f32[16,8,128]{2,1,0:T(8,128)S(1)}, u32[]{:S(2)}, u32[]{:S(2)}) collective-permute-start(f32[16,8,128]{2,1,0:T(8,128)S(1)} %all-to-all-done), channel_id=1, source_target_pairs={{0,2},{2,0},{1,3},{3,1},{4,6},{6,4},{5,7},{7,5},{8,10},{10,8},{9,1... | collective-permute-start | bytes 196616 | tf_op jit(solution)/shard_map/ppermute | solution.py:117
  58.1 4.8 %copy-start = (f32[512,128]{1,0:T(8,128)S(1)}, f32[512,128]{1,0:T(8,128)}, u32[]{:S(2)}) copy-start(f32[512,128]{1,0:T(8,128)} %param.7) | copy-start | bytes 786436
  58.1 4.8 %copy-start.1 = (f32[512,128]{1,0:T(8,128)S(1)}, f32[512,128]{1,0:T(8,128)}, u32[]{:S(2)}) copy-start(f32[512,128]{1,0:T(8,128)} %param.8) | copy-start | bytes 786436
  58.1 5.8 %collective-permute-start.1 = (f32[2,16,8,128]{3,2,1,0:T(8,128)S(1)}, f32[2,16,8,128]{3,2,1,0:T(8,128)S(1)}, u32[]{:S(2)}, u32[]{:S(2)}) collective-permute-start(f32[2,16,8,128]{3,2,1,0:T(8,128)S(1)} %pad_maximum_fusion.mine_ref), channel_id=1, source_target_pairs={{0,1},{1,0},{2,3},{3,2},{4,5},{5,4},{6,7},{7,6},{8,9},{9,8},{10,11... | collective-permute-start | bytes 393224 | tf_op jit(solution)/shard_map/ppermute | solution.py:134

commit v9 on v8

v9 whole, which is shorter than its diff:
```python
import math

import jax
import jax.numpy as jnp
from jax import lax
from jax.experimental import pallas as pl
from jax.experimental.pallas import tpu as pltpu
from jax.sharding import Mesh, PartitionSpec as P


ROW = ("x", "y")
COL = ("z_far", "z_lo", "core")
NEAR = (*ROW, "z_lo", "core")
ROW_FIRST = 2 * 4 + 2
NEAR_FIRST = (ROW_FIRST * 2 + 1) * 2
FAR_FIRST = 8


def dot(left, right):
    return jnp.dot(
        left,
        right,
        precision=lax.Precision.HIGHEST,
        preferred_element_type=jnp.float32,
    )


def kern_body(shift_ref, omega_ref, freq_ref, out_ref):
    rows, depth = out_ref.shape[2:]
    for core in range(out_ref.shape[0]):
        freq = freq_ref[:, core].reshape(rows, depth)
        ratio = omega_ref[:, core].reshape(rows, depth) / freq
        for energy in range(out_ref.shape[1]):
            gap = shift_ref[energy, 0:1, :] - freq
            out_ref[core, energy] = ratio * gap / (gap * gap + 0.09)


def half_terms(z_lo, core, kern_ref, blocks_ref, left_ref):
    chips = left_ref.shape[0]
    for i, at_z in enumerate((z_lo, 1 - z_lo)):
        left_ref[:FAR_FIRST, at_z] = blocks_ref[i, chips - FAR_FIRST :]
        left_ref[FAR_FIRST:, at_z] = blocks_ref[i, : chips - FAR_FIRST]
    left = left_ref[...].reshape(-1, left_ref.shape[-1]).T
    for energy in range(kern_ref.shape[1]):
        yield dot(left, kern_ref[core, energy])


def mine_body(place_ref, kern_ref, mine_ref, out_ref, left_ref):
    z_lo, core = place_ref[0], place_ref[1]
    for energy, term in enumerate(half_terms(z_lo, core, kern_ref, mine_ref, left_ref)):
        out_ref[energy] = term


def rest_body(place_ref, kern_ref, other_ref, part_ref, out_ref, left_ref):
    z_lo, core = place_ref[0], place_ref[1]
    for energy, term in enumerate(half_terms(z_lo, 1 - core, kern_ref, other_ref, left_ref)):
        out_ref[energy] = part_ref[energy] + term


def last_body(part_ref, right_ref, out_ref):
    lines, lanes = out_ref.shape[2:]
    for energy in range(part_ref.shape[0]):
        out_ref[:, energy] = dot(part_ref[energy], right_ref[...]).reshape(-1, lines, lanes)


def local_kernel(body, out_shape, flops, arrays, scratch=()):
    spaces = [pltpu.SMEM if a.dtype == jnp.int32 else pltpu.VMEM for a in arrays]
    return pl.pallas_call(
        body,
        out_shape=jax.ShapeDtypeStruct(out_shape, jnp.float32),
        in_specs=[pl.BlockSpec(memory_space=space) for space in spaces],
        out_specs=pl.BlockSpec(memory_space=pltpu.VMEM),
        scratch_shapes=scratch,
        compiler_params=pltpu.CompilerParams(vmem_limit_bytes=16 << 20),
        cost_estimate=pl.CostEstimate(
            flops=flops,
            bytes_accessed=4 * (sum(a.size for a in arrays) + math.prod(out_shape)),
            transcendentals=0,
        ),
    )(*arrays)


def exchange(pieces, axes, first):
    size = pieces.shape[0]
    order = [(first + i) % size for i in range(size)]
    return lax.all_to_all(pieces, axes, 0, 0, axis_index_groups=[order])


def gather(block, axes, first):
    size = lax.axis_size(axes)
    return exchange(jnp.broadcast_to(block, (size, *block.shape)), axes, first)


def sum_everywhere(tiles):
    size = lax.axis_size(NEAR)
    lanes = tiles.shape[-1]
    pieces = exchange(tiles.reshape(size, -1, 2, lanes), NEAR, NEAR_FIRST)
    piece = jnp.sum(gather(jnp.sum(pieces, axis=0), "z_far", FAR_FIRST), axis=0)
    return gather(piece, NEAR, NEAR_FIRST).reshape(tiles.shape)


def with_partner(blocks, axis):
    return jnp.stack([blocks, lax.ppermute(blocks, axis, ((0, 1), (1, 0)))])


def shards(omega_sq, pole_freq, mtx_left, mtx_right, band_ids, band_energy, eval_energy):
    table = band_energy.shape[0]
    energies = eval_energy.shape[0]
    states = mtx_left.shape[2]
    depth = pole_freq.shape[1]
    place = jnp.stack([lax.axis_index("z_lo"), lax.axis_index("core")])
    pairs = (-1, 2, mtx_left.shape[1], depth)
    omega, freq = omega_sq.reshape(pairs), pole_freq.reshape(pairs)
    hits = (band_ids[:, None] == jnp.arange(table, dtype=jnp.int32)[None, :]).astype(jnp.float32)
    levels = jnp.sum(hits * band_energy[None, :], axis=1)
    shifts = eval_energy[None, :] - levels[:, None]
    shift_rows = jnp.broadcast_to(shifts[0][:, None, None], (energies, 8, depth))
    left_far = gather(mtx_left[0], "z_far", FAR_FIRST)
    mine = with_partner(left_far, "z_lo")
    other = lax.ppermute(mine, "core", ((0, 1), (1, 0)))
    right_blocks = gather(mtx_right[0], ROW, ROW_FIRST)
    right_cols = jnp.roll(right_blocks, ROW_FIRST, axis=0).reshape(-1, states)
    shape = (2, energies, freq.size // depth // 2, depth)
    kern = local_kernel(kern_body, shape, 8 * energies * freq.size, (shift_rows, omega, freq))
    left_rows = pltpu.VMEM((mine.shape[1], mine.shape[0], *mine.shape[2:]), jnp.float32)
    flops = kern.size * states
    shape = (energies, states, depth)
    part = local_kernel(mine_body, shape, flops, (place, kern, mine), (left_rows,))
    part = local_kernel(rest_body, shape, flops, (place, kern, other, part), (left_rows,))
    shape = (states // 8, energies, 8, states)
    tiles = local_kernel(last_body, shape, 2 * part.size * states, (part, right_cols))
    return sum_everywhere(tiles).transpose(0, 2, 1, 3).reshape(states, energies * states)


def solution(mesh):
    split = Mesh(mesh.devices.reshape(4, 4, 16, 2, 2), (*ROW, *COL))
    return jax.shard_map(
        shards,
        mesh=split,
        in_specs=(
            P(ROW, COL),
            P(ROW, COL),
            P(None, (*ROW, *COL), None),
            P(None, (*COL, *ROW), None),
            P(),
            P(),
            P(),
        ),
        out_specs=P(),
        check_vma=False,
    )
```

time: 118 us -> 118 us (level)
    pallas_call x2 -> x4, Pallas kernels: 2.17 us -> 2.63 us  [local_kernel(): pl.pallas_call(body, out_shape=jax.ShapeDtypeStruct(out_shape, jnp.float3...]
where the time goes in v9:
time: 118 us; the launch traced here: 117 us
  blocking collectives  51.1 us (43%)
  starting transfers between devices  50.8 us (43%)
  waiting for transfers between devices  7.69 us (7%)
  local copies, waits for them, and re-layouts  2.83 us (2%)
  Pallas kernels  2.63 us (2%)
  other arithmetic  1.46 us (1%)
    all_to_all x3, blocking collectives, exchange(): return lax.all_to_all(pieces, axes, 0, 0, axis_index_groups=[order])  51.1 us
    all_to_all x2, starting transfers between devices, exchange(): return lax.all_to_all(pieces, axes, 0, 0, axis_index_groups=[order])  44.4 us
    all_to_all x2, waiting for transfers between devices, exchange(): return lax.all_to_all(pieces, axes, 0, 0, axis_index_groups=[order])  5.33 us
    ppermute x1, starting transfers between devices, shards(): other = lax.ppermute(mine, 'core', ((0, 1), (1, 0)))  4.42 us
    pallas_call x4, Pallas kernels, local_kernel(): pl.pallas_call(body, out_shape=jax.ShapeDtypeStruct(out_shape, jnp.float3...  2.63 us
  transfers between devices with their start and end apart: 4, of which 2 were waited for; matrix products, arithmetic and copies ran while one was open for 1% of the time, Pallas kernels for 1%

profile of v9, /device:TPU:1, one launch (start us, length us, event | category | flops | bytes accessed | tf_op | source)
XLA Modules:
  0.0 117.3 jit_solution(11826352491571819149)
XLA Ops:
  0.0 0.0 copy-start.3
  0.0 0.0 copy-start.2
  0.0 1.3 %broadcast_in_dim.11 = f32[16,8,128]{2,1,0:T(8,128)} broadcast(f32[8,128]{1,0:T(8,128)} %bitcast.24), dimensions={1,2} | broadcast | bytes 69632 | tf_op jit(solution)/shard_map/broadcast_in_dim | solution.py:91
  1.4 0.0 copy-start.4
  1.4 0.0 copy-start.1
  1.4 35.7 %all-to-all-start = ((f32[16,8,128]{2,1,0:T(8,128)}), f32[16,8,128]{2,1,0:T(8,128)S(1)}, u32[]{:S(2)}, u32[]{:S(2)}) async-start(f32[16,8,128]{2,1,0:T(8,128)} %broadcast_in_dim.11), calls=%async_computation | async-start | bytes 131072 | tf_op jit(solution)/shard_map/all_to_all | solution.py:86
  37.0 0.0 copy-start
  37.7 0.0 copy-done.3
  37.7 0.6 fusion
  38.4 5.3 %all-to-all-done = f32[16,8,128]{2,1,0:T(8,128)S(1)} async-done(((f32[16,8,128]{2,1,0:T(8,128)}), f32[16,8,128]{2,1,0:T(8,128)S(1)}, u32[]{:S(2)}, u32[]{:S(2)}) %all-to-all-start) | async-done | bytes 65568 | tf_op jit(solution)/shard_map/all_to_all | solution.py:86
  43.7 0.0 copy-done.2
  43.7 0.6 broadcast_in_dim.24
  44.3 8.7 %all-to-all-start.1 = ((f32[16,8,128]{2,1,0:T(8,128)}), f32[16,8,128]{2,1,0:T(8,128)S(1)}, u32[]{:S(2)}, u32[]{:S(2)}) async-start(f32[16,8,128]{2,1,0:T(8,128)} %broadcast_in_dim.24), calls=%async_computation.1 | async-start | bytes 131072 | tf_op jit(solution)/shard_map/all_to_all | solution.py:86
  53.0 2.0 %collective-permute-start = (f32[16,8,128]{2,1,0:T(8,128)S(1)}, f32[16,8,128]{2,1,0:T(8,128)S(1)}, u32[]{:S(2)}, u32[]{:S(2)}) collective-permute-start(f32[16,8,128]{2,1,0:T(8,128)S(1)} %all-to-all-done), channel_id=1, source_target_pairs={{0,2},{2,0},{1,3},{3,1},{4,6},{6,4},{5,7},{7,5},{8,10},{10,8},{9,1... | collective-permute-start | bytes 196616 | tf_op jit(solution)/shard_map/ppermute | solution.py:103
  55.0 0.0 copy-done.4
  55.1 0.6 broadcast_subtract_fusion
  55.7 2.4 %collective-permute-done = f32[16,8,128]{2,1,0:T(8,128)S(1)} collective-permute-done((f32[16,8,128]{2,1,0:T(8,128)S(1)}, f32[16,8,128]{2,1,0:T(8,128)S(1)}, u32[]{:S(2)}, u32[]{:S(2)}) %collective-permute-start) | collective-permute-done | bytes 65568 | tf_op jit(solution)/shard_map/ppermute | solution.py:103
  58.0 4.4 %collective-permute-start.1 = (f32[2,16,8,128]{3,2,1,0:T(8,128)S(1)}, f32[2,16,8,128]{3,2,1,0:T(8,128)S(1)}, u32[]{:S(2)}, u32[]{:S(2)}) collective-permute-start(f32[2,16,8,128]{3,2,1,0:T(8,128)S(1)} %pad_maximum_fusion.mine_ref), channel_id=1, source_target_pairs={{0,1},{1,0},{2,3},{3,2},{4,5},{5,4},{6,7},{7,6},{8,9},{9,8},{10,11... | collective-permute-start | bytes 393224 | tf_op jit(solution)/shard_map/ppermute | solution.py:120
  62.5 0.1 pad_add_fusion.place_ref
  62.5 0.1 broadcast_in_dim.10.shift_ref
  62.6 0.0 copy-done.1
  62.6 0.0 copy-done
  62.6 0.2 shard_map.73.kern_ref
  62.8 0.0 all-to-all-done.1
  62.9 1.1 shard_map.74.part_ref
  63.9 0.0 collective-permute-done.1.other_ref
  63.9 1.1 shard_map.75.part_ref
  65.0 0.3 shard_map.76
  65.3 11.8 %all_to_all.25 = f32[64,3,2,128]{3,2,1,0:T(2,128)S(1)} all-to-all(f32[64,3,2,128]{3,2,1,0:T(2,128)S(1)} %bitcast.18), channel_id=1, replica_groups={{642,643,704,705,706,707,768,769,770,771,832,833,834,835,896,897,898,89..., dimensions={0} | all-to-all | bytes 393216 | tf_op jit(solution)/shard_map/all_to_all | solution.py:86
  77.1 0.1 reduce_sum.28
  77.2 26.5 %all_to_all.26 = f32[16,3,2,128]{3,2,1,0:T(2,128)S(1)} all-to-all(f32[16,3,2,128]{3,2,1,0:T(2,128)S(1)} %broadcast_in_dim.25), channel_id=1, replica_groups={{32,36,40,44,48,52,56,60,0,4,8,12,16,20,24,28},{33,37,41,45,49,53,57,61..., dimensions={0} | all-to-all | bytes 98304 | tf_op jit(solution)/shard_map/all_to_all | solution.py:86
  103.7 0.1 broadcast_in_dim.26
  103.8 12.9 %all_to_all.27 = f32[64,3,2,128]{3,2,1,0:T(2,128)S(1)} all-to-all(f32[64,3,2,128]{3,2,1,0:T(2,128)S(1)} %broadcast_in_dim.26), channel_id=1, replica_groups={{642,643,704,705,706,707,768,769,770,771,832,833,834,835,896,897,898,89..., dimensions={0} | all-to-all | bytes 393216 | tf_op jit(solution)/shard_map/all_to_all | solution.py:86
  116.6 0.7 copy.12
  (6 shorter events, 0.1 us)
Async XLA Ops:
  0.0 37.7 %copy-start.3 = (f32[64]{0:T(128)S(1)}, f32[64]{0:T(128)}, u32[]{:S(2)}) copy-start(f32[64]{0:T(128)} %param.12) | copy-start | bytes 772
  0.0 43.7 %copy-start.2 = (f32[1,8,128]{2,1,0:T(8,128)S(1)}, f32[1,8,128]{2,1,0:T(8,128)}, u32[]{:S(2)}) copy-start(f32[1,8,128]{2,1,0:T(8,128)} %param.10) | copy-start | bytes 12292
  1.4 53.7 %copy-start.4 = (f32[3]{0:T(128)S(1)}, f32[3]{0:T(128)}, u32[]{:S(2)}) copy-start(f32[3]{0:T(128)} %param.13) | copy-start | bytes 40
  1.4 61.3 %copy-start.1 = (f32[512,128]{1,0:T(8,128)S(1)}, f32[512,128]{1,0:T(8,128)}, u32[]{:S(2)}) copy-start(f32[512,128]{1,0:T(8,128)} %param.8) | copy-start | bytes 786436
  1.4 42.3 %all-to-all-start = ((f32[16,8,128]{2,1,0:T(8,128)}), f32[16,8,128]{2,1,0:T(8,128)S(1)}, u32[]{:S(2)}, u32[]{:S(2)}) async-start(f32[16,8,128]{2,1,0:T(8,128)} %broadcast_in_dim.11), calls=%async_computation | async-start | bytes 131072 | tf_op jit(solution)/shard_map/all_to_all | solution.py:86
  37.0 25.6 %copy-start = (f32[512,128]{1,0:T(8,128)S(1)}, f32[512,128]{1,0:T(8,128)}, u32[]{:S(2)}) copy-start(f32[512,128]{1,0:T(8,128)} %param.7) | copy-start | bytes 786436
  44.3 18.5 %all-to-all-start.1 = ((f32[16,8,128]{2,1,0:T(8,128)}), f32[16,8,128]{2,1,0:T(8,128)S(1)}, u32[]{:S(2)}, u32[]{:S(2)}) async-start(f32[16,8,128]{2,1,0:T(8,128)} %broadcast_in_dim.24), calls=%async_computation.1 | async-start | bytes 131072 | tf_op jit(solution)/shard_map/all_to_all | solution.py:86
  53.0 5.0 %collective-permute-start = (f32[16,8,128]{2,1,0:T(8,128)S(1)}, f32[16,8,128]{2,1,0:T(8,128)S(1)}, u32[]{:S(2)}, u32[]{:S(2)}) collective-permute-start(f32[16,8,128]{2,1,0:T(8,128)S(1)} %all-to-all-done), channel_id=1, source_target_pairs={{0,2},{2,0},{1,3},{3,1},{4,6},{6,4},{5,7},{7,5},{8,10},{10,8},{9,1... | collective-permute-start | bytes 196616 | tf_op jit(solution)/shard_map/ppermute | solution.py:103
  58.0 5.9 %collective-permute-start.1 = (f32[2,16,8,128]{3,2,1,0:T(8,128)S(1)}, f32[2,16,8,128]{3,2,1,0:T(8,128)S(1)}, u32[]{:S(2)}, u32[]{:S(2)}) collective-permute-start(f32[2,16,8,128]{3,2,1,0:T(8,128)S(1)} %pad_maximum_fusion.mine_ref), channel_id=1, source_target_pairs={{0,1},{1,0},{2,3},{3,2},{4,5},{5,4},{6,7},{7,6},{8,9},{9,8},{10,11... | collective-permute-start | bytes 393224 | tf_op jit(solution)/shard_map/ppermute | solution.py:120

commit v10 on v9

--- a/solution.py
+++ b/solution.py
@@ -13,7 +13,7 @@
 NEAR = (*ROW, "z_lo", "core")
 ROW_FIRST = 2 * 4 + 2
 NEAR_FIRST = (ROW_FIRST * 2 + 1) * 2
-FAR_FIRST = 8
+FAR_FIRST = 9
 
 
 def dot(left, right):
@@ -26,41 +26,39 @@
 
 
 def kern_body(shift_ref, omega_ref, freq_ref, out_ref):
-    rows, depth = out_ref.shape[2:]
+    rows = out_ref.shape[1]
+    depth = freq_ref.shape[-1]
     for core in range(out_ref.shape[0]):
         freq = freq_ref[:, core].reshape(rows, depth)
         ratio = omega_ref[:, core].reshape(rows, depth) / freq
-        for energy in range(out_ref.shape[1]):
+        for energy in range(shift_ref.shape[0]):
             gap = shift_ref[energy, 0:1, :] - freq
-            out_ref[core, energy] = ratio * gap / (gap * gap + 0.09)
+            out_ref[core, :, energy * depth : (energy + 1) * depth] = ratio * gap / (gap * gap + 0.09)
 
 
-def half_terms(z_lo, core, kern_ref, blocks_ref, left_ref):
+def half_term(z_lo, core, kern_ref, blocks_ref, left_ref):
     chips = left_ref.shape[0]
     for i, at_z in enumerate((z_lo, 1 - z_lo)):
         left_ref[:FAR_FIRST, at_z] = blocks_ref[i, chips - FAR_FIRST :]
         left_ref[FAR_FIRST:, at_z] = blocks_ref[i, : chips - FAR_FIRST]
-    left = left_ref[...].reshape(-1, left_ref.shape[-1]).T
-    for energy in range(kern_ref.shape[1]):
-        yield dot(left, kern_ref[core, energy])
+    return dot(left_ref[...].reshape(-1, left_ref.shape[-1]).T, kern_ref[core])
 
 
 def mine_body(place_ref, kern_ref, mine_ref, out_ref, left_ref):
-    z_lo, core = place_ref[0], place_ref[1]
-    for energy, term in enumerate(half_terms(z_lo, core, kern_ref, mine_ref, left_ref)):
-        out_ref[energy] = term
+    out_ref[...] = half_term(place_ref[0], place_ref[1], kern_ref, mine_ref, left_ref)
 
 
 def rest_body(place_ref, kern_ref, other_ref, part_ref, out_ref, left_ref):
-    z_lo, core = place_ref[0], place_ref[1]
-    for energy, term in enumerate(half_terms(z_lo, 1 - core, kern_ref, other_ref, left_ref)):
-        out_ref[energy] = part_ref[energy] + term
+    term = half_term(place_ref[0], 1 - place_ref[1], kern_ref, other_ref, left_ref)
+    out_ref[...] = part_ref[...] + term
 
 
 def last_body(part_ref, right_ref, out_ref):
     lines, lanes = out_ref.shape[2:]
-    for energy in range(part_ref.shape[0]):
-        out_ref[:, energy] = dot(part_ref[energy], right_ref[...]).reshape(-1, lines, lanes)
+    depth = right_ref.shape[0]
+    for energy in range(out_ref.shape[1]):
+        part = part_ref[:, energy * depth : (energy + 1) * depth]
+        out_ref[:, energy] = dot(part, right_ref[...]).reshape(-1, lines, lanes)
 
 
 def local_kernel(body, out_shape, flops, arrays, scratch=()):
@@ -120,11 +118,11 @@
     other = lax.ppermute(mine, "core", ((0, 1), (1, 0)))
     right_blocks = gather(mtx_right[0], ROW, ROW_FIRST)
     right_cols = jnp.roll(right_blocks, ROW_FIRST, axis=0).reshape(-1, states)
-    shape = (2, energies, freq.size // depth // 2, depth)
+    shape = (2, freq.size // depth // 2, energies * depth)
     kern = local_kernel(kern_body, shape, 8 * energies * freq.size, (shift_rows, omega, freq))
     left_rows = pltpu.VMEM((mine.shape[1], mine.shape[0], *mine.shape[2:]), jnp.float32)
     flops = kern.size * states
-    shape = (energies, states, depth)
+    shape = (states, energies * depth)
     part = local_kernel(mine_body, shape, flops, (place, kern, mine), (left_rows,))
     part = local_kernel(rest_body, shape, flops, (place, kern, other, part), (left_rows,))
     shape = (states // 8, energies, 8, states)

time: 118 us -> 117 us (level)
  starting transfers between devices: 50.8 us -> 49.5 us
  waiting for transfers between devices: 7.69 us -> 8.94 us
    all_to_all x2, starting transfers between devices: 44.4 us -> 42.6 us  [exchange(): return lax.all_to_all(pieces, axes, 0, 0, axis_index_groups=[order])]
where the time goes in v10:
time: 117 us
  blocking collectives  51 us (44%)
  starting transfers between devices  49.5 us (42%)
  waiting for transfers between devices  8.94 us (8%)
  local copies, waits for them, and re-layouts  2.83 us (2%)
  Pallas kernels  2.44 us (2%)
  other arithmetic  1.46 us (1%)
    all_to_all x3, blocking collectives, exchange(): return lax.all_to_all(pieces, axes, 0, 0, axis_index_groups=[order])  51 us
    all_to_all x2, starting transfers between devices, exchange(): return lax.all_to_all(pieces, axes, 0, 0, axis_index_groups=[order])  42.6 us
    all_to_all x2, waiting for transfers between devices, exchange(): return lax.all_to_all(pieces, axes, 0, 0, axis_index_groups=[order])  6.48 us
    ppermute x1, starting transfers between devices, shards(): other = lax.ppermute(mine, 'core', ((0, 1), (1, 0)))  5.06 us
    ppermute x1, waiting for transfers between devices, with_partner(): return jnp.stack([blocks, lax.ppermute(blocks, axis, ((0, 1), (1, 0)))])  2.45 us
    pallas_call x4, Pallas kernels, local_kernel(): pl.pallas_call(body, out_shape=jax.ShapeDtypeStruct(out_shape, jnp.float3...  2.44 us
  transfers between devices with their start and end apart: 4, of which 2 were waited for; matrix products, arithmetic and copies ran while one was open for 1% of the time, Pallas kernels for 1%

profile of v10, /device:TPU:1, one launch (start us, length us, event | category | flops | bytes accessed | tf_op | source)
XLA Modules:
  0.0 117.0 jit_solution(11139082333442691430)
XLA Ops:
  0.0 0.0 copy-start.3
  0.0 0.0 copy-start.2
  0.0 1.3 %broadcast_in_dim.11 = f32[16,8,128]{2,1,0:T(8,128)} broadcast(f32[8,128]{1,0:T(8,128)} %bitcast.24), dimensions={1,2} | broadcast | bytes 69632 | tf_op jit(solution)/shard_map/broadcast_in_dim | solution.py:89
  1.4 0.0 copy-start.4
  1.4 0.0 copy-start.1
  1.4 33.9 %all-to-all-start = ((f32[16,8,128]{2,1,0:T(8,128)}), f32[16,8,128]{2,1,0:T(8,128)S(1)}, u32[]{:S(2)}, u32[]{:S(2)}) async-start(f32[16,8,128]{2,1,0:T(8,128)} %broadcast_in_dim.11), calls=%async_computation | async-start | bytes 131072 | tf_op jit(solution)/shard_map/all_to_all | solution.py:84
  35.2 0.0 copy-start
  35.9 0.0 copy-done.3
  35.9 0.6 fusion
  36.6 6.5 %all-to-all-done = f32[16,8,128]{2,1,0:T(8,128)S(1)} async-done(((f32[16,8,128]{2,1,0:T(8,128)}), f32[16,8,128]{2,1,0:T(8,128)S(1)}, u32[]{:S(2)}, u32[]{:S(2)}) %all-to-all-start) | async-done | bytes 65568 | tf_op jit(solution)/shard_map/all_to_all | solution.py:84
  43.1 0.0 copy-done.2
  43.1 0.6 broadcast_in_dim.24
  43.7 8.7 %all-to-all-start.1 = ((f32[16,8,128]{2,1,0:T(8,128)}), f32[16,8,128]{2,1,0:T(8,128)S(1)}, u32[]{:S(2)}, u32[]{:S(2)}) async-start(f32[16,8,128]{2,1,0:T(8,128)} %broadcast_in_dim.24), calls=%async_computation.1 | async-start | bytes 131072 | tf_op jit(solution)/shard_map/all_to_all | solution.py:84
  52.4 1.9 %collective-permute-start = (f32[16,8,128]{2,1,0:T(8,128)S(1)}, f32[16,8,128]{2,1,0:T(8,128)S(1)}, u32[]{:S(2)}, u32[]{:S(2)}) collective-permute-start(f32[16,8,128]{2,1,0:T(8,128)S(1)} %all-to-all-done), channel_id=1, source_target_pairs={{0,2},{2,0},{1,3},{3,1},{4,6},{6,4},{5,7},{7,5},{8,10},{10,8},{9,1... | collective-permute-start | bytes 196616 | tf_op jit(solution)/shard_map/ppermute | solution.py:101
  54.3 0.0 copy-done.4
  54.3 0.6 broadcast_subtract_fusion
  54.9 2.4 %collective-permute-done = f32[16,8,128]{2,1,0:T(8,128)S(1)} collective-permute-done((f32[16,8,128]{2,1,0:T(8,128)S(1)}, f32[16,8,128]{2,1,0:T(8,128)S(1)}, u32[]{:S(2)}, u32[]{:S(2)}) %collective-permute-start) | collective-permute-done | bytes 65568 | tf_op jit(solution)/shard_map/ppermute | solution.py:101
  57.4 5.1 %collective-permute-start.1 = (f32[2,16,8,128]{3,2,1,0:T(8,128)S(1)}, f32[2,16,8,128]{3,2,1,0:T(8,128)S(1)}, u32[]{:S(2)}, u32[]{:S(2)}) collective-permute-start(f32[2,16,8,128]{3,2,1,0:T(8,128)S(1)} %pad_maximum_fusion.mine_ref), channel_id=1, source_target_pairs={{0,1},{1,0},{2,3},{3,2},{4,5},{5,4},{6,7},{7,6},{8,9},{9,8},{10,11... | collective-permute-start | bytes 393224 | tf_op jit(solution)/shard_map/ppermute | solution.py:118
  62.5 0.1 pad_add_fusion.place_ref
  62.5 0.1 broadcast_in_dim.10.shift_ref
  62.6 0.0 copy-done.1
  62.6 0.0 copy-done
  62.6 0.2 shard_map.73.kern_ref
  62.8 0.0 all-to-all-done.1
  62.9 1.0 shard_map.74.part_ref
  63.8 0.0 collective-permute-done.1.other_ref
  63.9 1.0 shard_map.75.part_ref
  64.8 0.3 shard_map.76
  65.1 11.8 %all_to_all.25 = f32[64,3,2,128]{3,2,1,0:T(2,128)S(1)} all-to-all(f32[64,3,2,128]{3,2,1,0:T(2,128)S(1)} %bitcast.18), channel_id=1, replica_groups={{642,643,704,705,706,707,768,769,770,771,832,833,834,835,896,897,898,89..., dimensions={0} | all-to-all | bytes 393216 | tf_op jit(solution)/shard_map/all_to_all | solution.py:84
  76.9 0.1 reduce_sum.28
  77.0 24.5 %all_to_all.26 = f32[16,3,2,128]{3,2,1,0:T(2,128)S(1)} all-to-all(f32[16,3,2,128]{3,2,1,0:T(2,128)S(1)} %broadcast_in_dim.25), channel_id=1, replica_groups={{36,40,44,48,52,56,60,0,4,8,12,16,20,24,28,32},{37,41,45,49,53,57,61,1,..., dimensions={0} | all-to-all | bytes 98304 | tf_op jit(solution)/shard_map/all_to_all | solution.py:84
  101.6 0.1 broadcast_in_dim.26
  101.7 14.7 %all_to_all.27 = f32[64,3,2,128]{3,2,1,0:T(2,128)S(1)} all-to-all(f32[64,3,2,128]{3,2,1,0:T(2,128)S(1)} %broadcast_in_dim.26), channel_id=1, replica_groups={{642,643,704,705,706,707,768,769,770,771,832,833,834,835,896,897,898,89..., dimensions={0} | all-to-all | bytes 393216 | tf_op jit(solution)/shard_map/all_to_all | solution.py:84
  116.4 0.7 copy.12
  (6 shorter events, 0.1 us)
Async XLA Ops:
  0.0 35.9 %copy-start.3 = (f32[64]{0:T(128)S(1)}, f32[64]{0:T(128)}, u32[]{:S(2)}) copy-start(f32[64]{0:T(128)} %param.12) | copy-start | bytes 772
  0.0 43.1 %copy-start.2 = (f32[1,8,128]{2,1,0:T(8,128)S(1)}, f32[1,8,128]{2,1,0:T(8,128)}, u32[]{:S(2)}) copy-start(f32[1,8,128]{2,1,0:T(8,128)} %param.10) | copy-start | bytes 12292
  1.4 53.0 %copy-start.4 = (f32[3]{0:T(128)S(1)}, f32[3]{0:T(128)}, u32[]{:S(2)}) copy-start(f32[3]{0:T(128)} %param.13) | copy-start | bytes 40
  1.4 61.3 %copy-start.1 = (f32[512,128]{1,0:T(8,128)S(1)}, f32[512,128]{1,0:T(8,128)}, u32[]{:S(2)}) copy-start(f32[512,128]{1,0:T(8,128)} %param.8) | copy-start | bytes 786436
  1.4 41.7 %all-to-all-start = ((f32[16,8,128]{2,1,0:T(8,128)}), f32[16,8,128]{2,1,0:T(8,128)S(1)}, u32[]{:S(2)}, u32[]{:S(2)}) async-start(f32[16,8,128]{2,1,0:T(8,128)} %broadcast_in_dim.11), calls=%async_computation | async-start | bytes 131072 | tf_op jit(solution)/shard_map/all_to_all | solution.py:84
  35.2 27.4 %copy-start = (f32[512,128]{1,0:T(8,128)S(1)}, f32[512,128]{1,0:T(8,128)}, u32[]{:S(2)}) copy-start(f32[512,128]{1,0:T(8,128)} %param.7) | copy-start | bytes 786436
  43.7 19.1 %all-to-all-start.1 = ((f32[16,8,128]{2,1,0:T(8,128)}), f32[16,8,128]{2,1,0:T(8,128)S(1)}, u32[]{:S(2)}, u32[]{:S(2)}) async-start(f32[16,8,128]{2,1,0:T(8,128)} %broadcast_in_dim.24), calls=%async_computation.1 | async-start | bytes 131072 | tf_op jit(solution)/shard_map/all_to_all | solution.py:84
  52.4 5.0 %collective-permute-start = (f32[16,8,128]{2,1,0:T(8,128)S(1)}, f32[16,8,128]{2,1,0:T(8,128)S(1)}, u32[]{:S(2)}, u32[]{:S(2)}) collective-permute-start(f32[16,8,128]{2,1,0:T(8,128)S(1)} %all-to-all-done), channel_id=1, source_target_pairs={{0,2},{2,0},{1,3},{3,1},{4,6},{6,4},{5,7},{7,5},{8,10},{10,8},{9,1... | collective-permute-start | bytes 196616 | tf_op jit(solution)/shard_map/ppermute | solution.py:101
  57.4 6.4 %collective-permute-start.1 = (f32[2,16,8,128]{3,2,1,0:T(8,128)S(1)}, f32[2,16,8,128]{3,2,1,0:T(8,128)S(1)}, u32[]{:S(2)}, u32[]{:S(2)}) collective-permute-start(f32[2,16,8,128]{3,2,1,0:T(8,128)S(1)} %pad_maximum_fusion.mine_ref), channel_id=1, source_target_pairs={{0,1},{1,0},{2,3},{3,2},{4,5},{5,4},{6,7},{7,6},{8,9},{9,8},{10,11... | collective-permute-start | bytes 393224 | tf_op jit(solution)/shard_map/ppermute | solution.py:118
